TPU v7x, 256 devices: a whole 4x4x8 slice. The times are simulated.
256 devices in a mesh: seq: 8 (over x, core), expert: 32 (over z, y).
Axes of the slice: x: 4, y: 4, z: 8, core: 2. Of those that a mesh axis runs over, the one named last changes fastest.
Arguments:
- queries: bfloat16 [2, 2048, 8192], P(None, 'seq', 'expert'), may hold values from -6 to 6
- key_rows: bfloat16 [2, 2048, 8192], P(None, 'seq', 'expert'), may hold values from -6 to 6
- value_rows: bfloat16 [2, 2048, 8192], P(None, 'seq', 'expert'), may hold values from -6 to 6
- decay_rate: float32 [64], P('expert'), as said below
- norm_gain: float32 [8192], P('expert'), may hold values from 0.1 to 1.9
- attn_probe: bfloat16 [2, 2048, 8192], P(None, 'seq', 'expert'), may hold values from -6 to 6
- hidden_in: bfloat16 [2, 2048, 6144], P(None, ('seq', 'expert')), may hold values from -6 to 6
- moe_probe: bfloat16 [2, 2048, 6144], P(None, ('seq', 'expert')), may hold values from -6 to 6
- router_weight: bfloat16 [6144, 4], replicated, may hold values from -0.078125 to 0.078125
- routes: int32 [2, 2048, 2], P(None, ('seq', 'expert')), may hold values from 0 to 3, all different within a row; in each aligned block of 8 rows (0 to 7, 8 to 15, ..., all dimensions but the last counted through in order) at most 5 rows name the same one
- gate_weight: bfloat16 [32, 6144, 576], P('expert', 'seq'), may hold values from -0.078125 to 0.078125
- up_weight: bfloat16 [32, 6144, 576], P('expert', 'seq'), may hold values from -0.078125 to 0.078125
- down_weight: bfloat16 [32, 6144, 576], P('expert', 'seq'), may hold values from -0.09375 to 0.09375
- rollout_logprob: float32 [2, 2048], P(None, 'seq'), may hold values from -1 to 0
- trainer_logprob: float32 [2, 2048], P(None, 'seq'), may hold values from -1 to 0
- advantage: float32 [2, 2048], P(None, 'seq'), may hold values from -4 to 4
- clip_low: float32 [1], replicated, may hold values from 0.4 to 0.95
- clip_high: float32 [1], replicated, may hold values from 1.05 to 2.5
Outputs:
- objective: float32 [2, 2048], P(None, 'seq')
- grad_queries: bfloat16 [2, 2048, 8192], P(None, 'seq', 'expert')
- grad_keys: bfloat16 [2, 2048, 8192], P(None, 'seq', 'expert')
- grad_values: bfloat16 [2, 2048, 8192], P(None, 'seq', 'expert')
- grad_hidden: bfloat16 [2, 2048, 6144], P(None, ('seq', 'expert'))
Inputs may be any that keep to these rules, and one draw needn't show every extreme that they name: `routes`: in each rollout, the 8 positions that one device holds in the expert block name no expert more than 5 times; the 2 experts of a token differ. `decay_rate`: positive rates.
All inputs are finite; a program needn't handle non-finite values.
Results may differ from a plain program's by a relative error of at most 0.0045.
The roundings to bfloat16 on the way count: a program that leaves them out, or rounds other values in their place, can miss the bound.
Values may be sent and summed in bfloat16 or wider, within the bound.
A program may use at most 128 MiB of HBM per device.

v0:
```python
import jax
import jax.numpy as jnp
from jax import lax
from jax.sharding import PartitionSpec as P

highest = lax.Precision.HIGHEST
norm_epsilon = 1e-06


def entering(x, axis, combine, identity, reverse):
    length, here = (lax.axis_size(axis), lax.axis_index(axis))
    everything = jax.tree.map(lambda part: lax.all_gather(part, axis), x)
    start = jax.tree.map(
        lambda part, zero: jnp.broadcast_to(jnp.asarray(zero, part.dtype), part.shape), x, identity
    )

    def lap(k, before):
        at = length - 1 - k if reverse else k
        reached = at > here if reverse else at < here
        new = combine(before, jax.tree.map(lambda part: part[at], everything))
        return jax.tree.map(lambda a, b: jnp.where(reached, a, b), new, before)

    return lax.fori_loop(0, length, lap, start)


def carry_combine(earlier, later):
    return (earlier[0] * later[0], later[0] * earlier[1] + later[1])


def earlier_state(summary, block_decay):
    identity = (jnp.ones_like(block_decay), jnp.zeros_like(summary))
    result = entering((block_decay, summary), "seq", carry_combine, identity, False)
    return result[1]


def later_state(summary, block_decay):
    identity = (jnp.ones_like(block_decay), jnp.zeros_like(summary))
    result = entering((block_decay, summary), "seq", carry_combine, identity, True)
    return result[1]


def on_device(
    queries,
    key_rows,
    value_rows,
    decay_rate,
    norm_gain,
    attn_probe,
    hidden_in,
    moe_probe,
    router_weight,
    routes,
    gate_weight,
    up_weight,
    down_weight,
    rollout_logprob,
    trainer_logprob,
    advantage,
    clip_low,
    clip_high,
):
    rollouts, block_size, feature_width = queries.shape
    head_count = decay_rate.shape[0]
    head_size = feature_width // head_count
    importance = jnp.exp(trainer_logprob - rollout_logprob)
    clipped = jnp.minimum(jnp.maximum(importance, clip_low[0]), clip_high[0])
    coeff = -(clipped * advantage) / rollouts
    objective = coeff * trainer_logprob
    gate_block, up_block, down_block = (
        lax.all_gather(gate_weight, "seq", axis=1, tiled=True),
        lax.all_gather(up_weight, "seq", axis=1, tiled=True),
        lax.all_gather(down_weight, "seq", axis=1, tiled=True),
    )
    gate_mat = gate_block[0]
    up_mat = up_block[0]
    down_mat = down_block[0]
    shape_four = (rollouts, block_size, head_count, head_size)
    query_full = queries.reshape(shape_four).astype(jnp.float32)
    key_full = key_rows.reshape(shape_four).astype(jnp.float32)
    value_full = value_rows.reshape(shape_four).astype(jnp.float32)
    probe_full = attn_probe.reshape(shape_four).astype(jnp.float32)
    gain_full = norm_gain.reshape(head_count, head_size)
    offsets = jnp.arange(block_size, dtype=jnp.float32)
    rate_row = decay_rate[None, :]
    distance = offsets[:, None] - offsets[None, :]
    within = jnp.where(
        (distance >= 0)[None],
        jnp.exp(-decay_rate[:, None, None] * jnp.maximum(distance, 0.0)[None]),
        0.0,
    )
    lead_decay = jnp.exp(-rate_row * (offsets[:, None] + 1.0))[None, :, :, None]
    key_tail = jnp.exp(-rate_row * (block_size - 1.0 - offsets[:, None]))[None, :, :, None]
    query_tail = jnp.exp(-rate_row * offsets[:, None])[None, :, :, None]
    grad_tail = jnp.exp(-rate_row * (block_size - offsets[:, None]))[None, :, :, None]
    block_decay = jnp.exp(-decay_rate * block_size).reshape(1, head_count, 1, 1)
    forward_summary = jnp.einsum(
        "rjhk,rjhv->rhkv", key_full * key_tail, value_full, precision=highest
    )
    state_before = earlier_state(forward_summary, block_decay)
    scores = jnp.einsum("rihc,rjhc->rhij", query_full, key_full, precision=highest) * within[None]
    output = jnp.einsum("rhij,rjhv->rihv", scores, value_full, precision=highest)
    output = output + lead_decay * jnp.einsum(
        "rihk,rhkv->rihv", query_full, state_before, precision=highest
    )
    inverse = lax.rsqrt(jnp.mean(output * output, axis=-1, keepdims=True) + norm_epsilon)
    scaled = gain_full[None, None] * (coeff[:, :, None, None] * probe_full)
    grad_out = inverse * scaled - output * inverse**3 * jnp.mean(
        scaled * output, axis=-1, keepdims=True
    )
    backward_summary = jnp.einsum(
        "rihk,rihv->rhkv", query_full * query_tail, grad_out, precision=highest
    )
    state_after = later_state(backward_summary, block_decay)
    product = jnp.einsum("rihv,rjhv->rhij", grad_out, value_full, precision=highest) * within[None]
    grad_query = jnp.einsum("rhij,rjhk->rihk", product, key_full, precision=highest)
    grad_query = grad_query + lead_decay * jnp.einsum(
        "rihv,rhkv->rihk", grad_out, state_before, precision=highest
    )
    grad_key = jnp.einsum("rhij,rihk->rjhk", product, query_full, precision=highest)
    grad_key = grad_key + grad_tail * jnp.einsum(
        "rjhv,rhkv->rjhk", value_full, state_after, precision=highest
    )
    grad_value = jnp.einsum("rhij,rihv->rjhv", scores, grad_out, precision=highest)
    grad_value = grad_value + grad_tail * jnp.einsum(
        "rjhk,rhkv->rjhv", key_full, state_after, precision=highest
    )
    out_shape = (rollouts, block_size, feature_width)
    grad_queries = grad_query.reshape(out_shape).astype(jnp.bfloat16)
    grad_keys = grad_key.reshape(out_shape).astype(jnp.bfloat16)
    grad_values = grad_value.reshape(out_shape).astype(jnp.bfloat16)
    expert_count = lax.axis_size("expert")
    expert_index = lax.axis_index("expert")
    window_experts = router_weight.shape[1]
    slice_count = expert_count // window_experts
    positions = hidden_in.shape[1]
    top_count = routes.shape[2]
    model_width = hidden_in.shape[2]
    capacity = positions // 2 + 1
    local_coeff = lax.dynamic_slice_in_dim(coeff, expert_index * positions, positions, 1)
    grad_rows = (local_coeff[:, :, None] * moe_probe.astype(jnp.float32)).astype(jnp.bfloat16)
    onehot = (routes[..., None] == jnp.arange(window_experts, dtype=jnp.int32)).astype(jnp.float32)
    flat_hot = onehot.reshape(rollouts, positions * top_count, window_experts)
    earlier_count = jnp.cumsum(flat_hot, axis=1) - flat_hot
    slot_rank = jnp.sum(earlier_count * flat_hot, axis=-1)
    slot_hot = (slot_rank[..., None] == jnp.arange(capacity, dtype=jnp.float32)).astype(jnp.float32)
    select = (
        (flat_hot[..., None] * slot_hot[:, :, None, :])
        .reshape(rollouts, positions, top_count, window_experts, capacity)
        .sum(axis=2)
    )
    select_half = select.astype(jnp.bfloat16)
    token_buffer = jnp.einsum(
        "rpem,rpd->ermd", select_half, hidden_in, preferred_element_type=jnp.float32
    ).astype(jnp.bfloat16)
    grad_buffer = jnp.einsum(
        "rpem,rpd->ermd", select_half, grad_rows, preferred_element_type=jnp.float32
    ).astype(jnp.bfloat16)

    def spread(buffer):
        wide = jnp.broadcast_to(
            buffer[:, None], (window_experts, slice_count, rollouts, capacity, model_width)
        )
        return wide.reshape(window_experts * slice_count, rollouts * capacity, model_width)

    token_part = lax.all_to_all(
        spread(token_buffer), "expert", split_axis=0, concat_axis=0, tiled=True
    )
    grad_part = lax.all_to_all(
        spread(grad_buffer), "expert", split_axis=0, concat_axis=0, tiled=True
    )
    sources, item_count, feature_count = token_part.shape
    token_flat = token_part.reshape(sources * item_count, feature_count)
    grad_flat = grad_part.reshape(sources * item_count, feature_count)
    pre_gate = jnp.dot(token_flat, gate_mat, preferred_element_type=jnp.float32)
    pre_up = jnp.dot(token_flat, up_mat, preferred_element_type=jnp.float32)
    sigmoid_gate = jax.nn.sigmoid(pre_gate)
    activated = pre_gate * sigmoid_gate
    units = activated * pre_up
    unit_grad = jnp.dot(grad_flat, down_mat, preferred_element_type=jnp.float32)
    slice_score = jnp.sum(units * unit_grad, axis=-1).astype(jnp.bfloat16)
    up_grad = (unit_grad * activated).astype(jnp.bfloat16)
    gate_grad = (
        unit_grad * pre_up * sigmoid_gate * (1.0 + pre_gate * (1.0 - sigmoid_gate))
    ).astype(jnp.bfloat16)
    contract = (((1,), (1,)), ((), ()))
    slice_dx = lax.dot_general(gate_grad, gate_mat, contract, preferred_element_type=jnp.float32)
    slice_dx = slice_dx + lax.dot_general(
        up_grad, up_mat, contract, preferred_element_type=jnp.float32
    )
    slice_dx = slice_dx.astype(jnp.bfloat16).reshape(sources, item_count, feature_count)
    returned_dx = lax.all_to_all(slice_dx, "expert", split_axis=0, concat_axis=0, tiled=True)
    returned_score = lax.all_to_all(
        slice_score.reshape(sources, item_count), "expert", split_axis=0, concat_axis=0, tiled=True
    )
    part_dx = (
        returned_dx.astype(jnp.float32)
        .reshape(window_experts, slice_count, rollouts, capacity, model_width)
        .sum(axis=1)
    )
    part_score = (
        returned_score.astype(jnp.float32)
        .reshape(window_experts, slice_count, rollouts, capacity)
        .sum(axis=1)
    )
    row_dx = jnp.einsum("rpem,ermd->rped", select, part_dx, precision=highest)
    row_score = jnp.einsum("rpem,erm->rpe", select, part_score, precision=highest)
    logits = jnp.einsum("rpd,de->rpe", hidden_in, router_weight, preferred_element_type=jnp.float32)
    chosen = jnp.einsum("rpke,rpe->rpk", onehot, logits, precision=highest)
    exponent = jnp.exp(chosen)
    gates = exponent / jnp.sum(exponent, axis=-1, keepdims=True)
    gate_expert = jnp.einsum("rpk,rpke->rpe", gates, onehot, precision=highest)
    score_pick = jnp.einsum("rpke,rpe->rpk", onehot, row_score, precision=highest)
    score_mean = jnp.sum(gates * score_pick, axis=-1, keepdims=True)
    logit_grad = gates * (score_pick - score_mean)
    logit_expert = jnp.einsum("rpk,rpke->rpe", logit_grad, onehot, precision=highest)
    grad_hidden = jnp.einsum("rpe,rped->rpd", gate_expert, row_dx, precision=highest)
    grad_hidden = grad_hidden + jnp.einsum(
        "rpe,de->rpd", logit_expert, router_weight.astype(jnp.float32), precision=highest
    )
    return (objective, grad_queries, grad_keys, grad_values, grad_hidden.astype(jnp.bfloat16))


def solution(mesh):
    in_specs = (
        P(None, "seq", "expert"),
        P(None, "seq", "expert"),
        P(None, "seq", "expert"),
        P("expert"),
        P("expert"),
        P(None, "seq", "expert"),
        P(None, ("seq", "expert"), None),
        P(None, ("seq", "expert"), None),
        P(),
        P(None, ("seq", "expert"), None),
        P("expert", "seq", None),
        P("expert", "seq", None),
        P("expert", "seq", None),
        P(None, "seq"),
        P(None, "seq"),
        P(None, "seq"),
        P(),
        P(),
    )
    out_specs = (
        P(None, "seq"),
        P(None, "seq", "expert"),
        P(None, "seq", "expert"),
        P(None, "seq", "expert"),
        P(None, ("seq", "expert"), None),
    )
    return jax.shard_map(
        on_device, mesh=mesh, in_specs=in_specs, out_specs=out_specs, check_vma=False
    )
```

profile of v0, /device:TPU:6, one launch (start us, length us, event | category | flops | bytes accessed | tf_op | source)
XLA Modules:
  0.0 566.0 jit_solution(8925561557179389963)
XLA Ops:
  7.3 1.1 copy.306
  8.4 1.3 dynamic-slice
  11.2 1.1 fusion.33
  17.1 1.3 fusion.72
  18.5 1.3 fusion.12
  20.9 5.0 copy.212
  25.9 11.7 %all-to-all-start = ((bf16[32,10,6144]{2,1,0:T(8,128)(2,1)}), bf16[32,10,6144]{2,1,0:T(8,128)(2,1)}, u32[]{:S(2)}, u32[]{:S(2)}) async-start(bf16[32,10,6144]{2,1,0:T(8,128)(2,1)} %copy.212), calls=%async_computation | async-start | bytes 12582912 | tf_op jit(solution)/shard_map/all_to_all | solution.py:168
  39.6 5.0 copy.215
  44.6 131.2 %all-to-all-done = bf16[32,10,6144]{2,1,0:T(8,128)(2,1)} async-done(((bf16[32,10,6144]{2,1,0:T(8,128)(2,1)}), bf16[32,10,6144]{2,1,0:T(8,128)(2,1)}, u32[]{:S(2)}, u32[]{:S(2)}) %all-to-all-start) | async-done | bytes 3932192 | tf_op jit(solution)/shard_map/all_to_all | solution.py:168
  175.9 14.6 %all-to-all-start.1 = ((bf16[32,10,6144]{2,1,0:T(8,128)(2,1)}), bf16[32,10,6144]{2,1,0:T(8,128)(2,1)}, u32[]{:S(2)}, u32[]{:S(2)}) async-start(bf16[32,10,6144]{2,1,0:T(8,128)(2,1)} %copy.215), calls=%async_computation.1 | async-start | bytes 12582912 | tf_op jit(solution)/shard_map/all_to_all | solution.py:165
  190.5 11.0 %all-reduce = f32[16]{0:T(128)S(1)} all-reduce(f32[16]{0:T(128)S(1)} %get-tuple-element.396), channel_id=2, replica_groups=mesh['seq'=8,'expert'=32] {'seq'}, use_global_device_ids=true, to_apply=%add | all-reduce | flops 16 | bytes 128
  202.6 8.7 %while.30 = (s32[]{:T(128)}, f32[2,2,128,128]{3,2,1,0:T(8,128)S(1)}, s32[]{:T(128)}, f32[8,1,2,1,1]{2,4,3,1,0:T(1,128)S(1)}, f32[8,2,2,128,128]{4,3,2,1,0:T(8,128)}, /*index=5*/s32[]{:T(128)}, s32[]{:T(128)}) while((s32[]{:T(128)}, f32[2,2,128,128]{3,2,1,0:T(8,128)S(1)}, s32[]{:T(128)}, f32[8,1,2,1,1]{2,4,3,1,0:T(1,128)S(1)}, ...), condition=%wide.region_1.2_spmd.clone, body=%wide.region_0.1_spmd.clone.sunk | while | flops 262148 | bytes 786561 | solution.py:23
  202.6 1.1 fusion.105
  203.7 1.1 fusion.105
  204.8 1.1 fusion.105
  205.9 1.1 fusion.105
  212.7 1.4 fusion.30
  214.2 7.6 %reshape.273 = bf16[320,6144]{1,0:T(8,128)(2,1)} reshape(bf16[32,10,6144]{2,1,0:T(8,128)(2,1)} %all-to-all-done) | data formatting | bytes 7864320 | tf_op jit(solution)/shard_map/reshape | solution.py:173
  221.7 109.8 %all-to-all-done.1 = bf16[32,10,6144]{2,1,0:T(8,128)(2,1)} async-done(((bf16[32,10,6144]{2,1,0:T(8,128)(2,1)}), bf16[32,10,6144]{2,1,0:T(8,128)(2,1)}, u32[]{:S(2)}, u32[]{:S(2)}) %all-to-all-start.1) | async-done | bytes 3932192 | tf_op jit(solution)/shard_map/all_to_all | solution.py:165
  331.6 7.6 %reshape.275 = bf16[320,6144]{1,0:T(8,128)(2,1)} reshape(bf16[32,10,6144]{2,1,0:T(8,128)(2,1)} %all-to-all-done.1) | data formatting | bytes 7864320 | tf_op jit(solution)/shard_map/reshape | solution.py:172
  339.2 7.4 %fusion.5 = f32[320,576]{1,0:T(8,128)S(1)} fusion(bf16[320,6144]{1,0:T(8,128)(2,1)} %reshape.275, bf16[1,6144,576]{1,2,0:T(8,128)(2,1)} %all-gather.13.cloned.1.call-done), kind=kOutput, calls=%fused_computation.11 | convolution fusion | flops 2264924160 | bytes 11747328 | tf_op jit(solution)/shard_map/dot_general | solution.py:174
  346.6 8.4 %fusion.8 = f32[320,576]{1,0:T(8,128)} fusion(bf16[320,6144]{1,0:T(8,128)(2,1)} %reshape.275, bf16[1,6144,576]{1,2,0:T(8,128)(2,1)} %all-gather.11.cloned.1.call-done), kind=kOutput, calls=%fused_computation.14 | convolution fusion | flops 2264924160 | bytes 11747328 | tf_op jit(solution)/shard_map/dot_general | solution.py:175
  355.0 8.4 %multiply_reduce_fusion = (bf16[320]{0:T(512)(128)(2,1)S(1)}, f32[320,576]{1,0:T(8,128)}) fusion(f32[320,576]{1,0:T(8,128)} %fusion.8, f32[320,576]{1,0:T(8,128)S(1)} %fusion.5, bf16[320,6144]{1,0:T(8,128)(2,1)} %reshape.273, bf16[1,6144,576]{1,2,0:T(8,128)(2,1)} %all-gather.9.cloned.1.call-done), kind=kOutput, calls=%fused_computation.49 | convolution fusion | flops 2266214144 | bytes 13222528 | tf_op jit(solution)/shard_map/dot_general | solution.py:179
  364.2 11.3 %all-to-all-start.3 = ((bf16[32,1,10]{2,1,0:T(2,128)(2,1)}), bf16[32,1,10]{2,1,0:T(2,128)(2,1)S(1)}, u32[]{:S(2)}, u32[]{:S(2)}) async-start(bf16[32,1,10]{2,1,0:T(2,128)(2,1)} %convert_element_type.138), calls=%async_computation.3 | async-start | bytes 32768 | tf_op jit(solution)/shard_map/all_to_all | solution.py:192
  375.6 6.8 %fusion.3 = f32[320,6144]{1,0:T(8,128)S(1)} fusion(bf16[1,6144,576]{1,2,0:T(8,128)(2,1)} %all-gather.13.cloned.1.call-done, f32[320,576]{1,0:T(8,128)S(1)} %fusion.5, f32[320,576]{1,0:T(8,128)} %get-tuple-element.399, f32[320,576]{1,0:T(8,128)} %fusion.8), kind=kOutput, calls=%fused_computation.9 | convolution fusion | flops 2266767360 | bytes 17154048 | tf_op jit(solution)/shard_map/dot_general | solution.py:186
  382.4 4.9 fusion.2
  387.2 7.4 %reshape.276 = bf16[32,10,6144]{2,1,0:T(8,128)(2,1)} reshape(bf16[320,6144]{1,0:T(8,128)(2,1)} %fusion.2) | data formatting | bytes 7864320 | tf_op jit(solution)/shard_map/reshape | solution.py:190
  394.6 10.0 %all-to-all-start.2 = ((bf16[32,10,6144]{2,1,0:T(8,128)(2,1)}), bf16[32,10,6144]{2,1,0:T(8,128)(2,1)}, u32[]{:S(2)}, u32[]{:S(2)}) async-start(bf16[32,10,6144]{2,1,0:T(8,128)(2,1)} %reshape.276), calls=%async_computation.2 | async-start | bytes 12582912 | tf_op jit(solution)/shard_map/all_to_all | solution.py:191
  405.8 1.7 convolution_multiply_fusion
  407.5 1.7 fusion.26
  410.0 18.8 %while.31 = (s32[]{:T(128)}, f32[2,2,128,128]{3,2,1,0:T(8,128)S(1)}, s32[]{:T(128)}, f32[8,1,2,1,1]{2,4,3,1,0:T(1,128)S(1)}, f32[8,2,2,128,128]{4,3,2,1,0:T(8,12...) while((s32[]{:T(128)}, f32[2,2,128,128]{3,2,1,0:T(8,128)S(1)}, s32[]{:T(128)}, ...), condition=%wide.region_5.6_spmd.clone, body=%wide.region_4.5_spmd.clone.sunk | while | flops 262152 | bytes 786623 | solution.py:23
  410.0 1.1 fusion.106
  411.2 1.1 fusion.106
  412.3 1.1 fusion.106
  413.4 1.1 fusion.106
  414.5 1.1 fusion.106
  415.6 1.1 fusion.106
  416.7 1.1 fusion.106
  417.8 1.1 fusion.106
  428.8 1.4 fusion.24
  430.2 1.5 fusion.28
  431.7 1.8 copy.223
  436.0 108.8 %all-to-all-done.2 = bf16[32,10,6144]{2,1,0:T(8,128)(2,1)} async-done(((bf16[32,10,6144]{2,1,0:T(8,128)(2,1)}), bf16[32,10,6144]{2,1,0:T(8,128)(2,1)}, u32[]{:S(2)}, u32[]{:S(2)}) %all-to-all-start.2) | async-done | bytes 3932192 | tf_op jit(solution)/shard_map/all_to_all | solution.py:191
  544.8 4.9 copy.216
  549.7 2.8 convert_reduce_fusion
  552.6 2.0 convolution_bitcast_fusion
  554.6 3.6 fusion.15
  558.2 1.1 fusion.14
  (121 shorter events, 19.4 us)
Async XLA Ops:
  7.2 4.0 copy-start
  7.2 195.4 %all-gather.15.cloned.1.call-start = ((), (), s32[]{:S(2)}) async-start(), calls=%async_computation.7 | async-start | bytes 2359296 | tf_op jit(solution)/shard_map/all_gather | solution.py:12
  8.3 12.5 %copy-start.4 = (bf16[2,256,256]{1,2,0:T(8,128)(2,1)}, bf16[2,256,256]{1,2,0:T(8,128)(2,1)S(1)}, u32[]{:S(2)}) copy-start(bf16[2,256,256]{1,2,0:T(8,128)(2,1)S(1)} %copy.306) | copy-start | bytes 786436
  12.3 326.9 %all-gather.13.cloned.1.call-start = ((), (), s32[]{:S(2)}) async-start(), calls=%async_computation.6 | async-start | bytes 7962624 | tf_op jit(solution)/shard_map/all_gather | solution.py:70
  13.1 333.6 %all-gather.11.cloned.1.call-start = ((), (), s32[]{:S(2)}) async-start(), calls=%async_computation.5 | async-start | bytes 7962624 | tf_op jit(solution)/shard_map/all_gather | solution.py:71
  25.9 12.3 %copy-start.9 = (bf16[2,8,6144]{2,1,0:T(8,128)(2,1)S(1)}, bf16[2,8,6144]{2,1,0:T(8,128)(2,1)}, u32[]{:S(2)}) copy-start(bf16[2,8,6144]{2,1,0:T(8,128)(2,1)} %param.28) | copy-start | bytes 589828
  25.9 149.9 %all-to-all-start = ((bf16[32,10,6144]{2,1,0:T(8,128)(2,1)}), bf16[32,10,6144]{2,1,0:T(8,128)(2,1)}, u32[]{:S(2)}, u32[]{:S(2)}) async-start(bf16[32,10,6144]{2,1,0:T(8,128)(2,1)} %copy.212), calls=%async_computation | async-start | bytes 12582912 | tf_op jit(solution)/shard_map/all_to_all | solution.py:168
  37.7 317.4 %all-gather.9.cloned.1.call-start = ((), (), s32[]{:S(2)}) async-start(), calls=%async_computation.4 | async-start | bytes 7962624 | tf_op jit(solution)/shard_map/all_gather | solution.py:72
  44.6 157.0 %copy-start.8 = (bf16[2,256,256]{2,1,0:T(8,128)(2,1)S(1)}, bf16[2,256,256]{2,1,0:T(8,128)(2,1)}, u32[]{:S(2)}) copy-start(bf16[2,256,256]{2,1,0:T(8,128)(2,1)} %param.22) | copy-start | bytes 786436
  44.6 157.1 %copy-start.7 = (bf16[2,256,256]{2,1,0:T(8,128)(2,1)S(1)}, bf16[2,256,256]{2,1,0:T(8,128)(2,1)}, u32[]{:S(2)}) copy-start(bf16[2,256,256]{2,1,0:T(8,128)(2,1)} %param.27) | copy-start | bytes 786436
  44.6 157.6 %copy-start.5 = (bf16[2,256,256]{2,1,0:T(8,128)(2,1)S(1)}, bf16[2,256,256]{2,1,0:T(8,128)(2,1)}, u32[]{:S(2)}) copy-start(bf16[2,256,256]{2,1,0:T(8,128)(2,1)} %param.23) | copy-start | bytes 786436
  175.9 155.7 %all-to-all-start.1 = ((bf16[32,10,6144]{2,1,0:T(8,128)(2,1)}), bf16[32,10,6144]{2,1,0:T(8,128)(2,1)}, u32[]{:S(2)}, u32[]{:S(2)}) async-start(bf16[32,10,6144]{2,1,0:T(8,128)(2,1)} %copy.215), calls=%async_computation.1 | async-start | bytes 12582912 | tf_op jit(solution)/shard_map/all_to_all | solution.py:165
  190.5 219.5 %all-gather.17.cloned.1.call-start = ((), (), s32[]{:S(2)}) async-start(), calls=%async_computation.8 | async-start | bytes 2359296 | tf_op jit(solution)/shard_map/all_gather | solution.py:12
  201.7 11.0 %copy-start.1 = (bf16[2,256,256]{1,2,0:T(8,128)(2,1)}, bf16[2,256,256]{1,2,0:T(8,128)(2,1)S(1)}, u32[]{:S(2)}) copy-start(bf16[2,256,256]{1,2,0:T(8,128)(2,1)S(1)} %copy.266) | copy-start | bytes 786436
  202.0 9.7 %copy-start.13 = (f32[256]{0:T(256)S(1)}, f32[256]{0:T(256)}, u32[]{:S(2)}) copy-start(f32[256]{0:T(256)} %param.26) | copy-start | bytes 3076
  202.2 10.4 %copy-start.3 = (f32[2,256,256]{2,1,0:T(8,128)}, f32[2,256,256]{2,1,0:T(8,128)S(1)}, u32[]{:S(2)}) copy-start(f32[2,256,256]{2,1,0:T(8,128)S(1)} %exponential_select_fusion) | copy-start | bytes 1572868
  364.2 30.4 %all-to-all-start.3 = ((bf16[32,1,10]{2,1,0:T(2,128)(2,1)}), bf16[32,1,10]{2,1,0:T(2,128)(2,1)S(1)}, u32[]{:S(2)}, u32[]{:S(2)}) async-start(bf16[32,1,10]{2,1,0:T(2,128)(2,1)} %convert_element_type.138), calls=%async_computation.3 | async-start | bytes 32768 | tf_op jit(solution)/shard_map/all_to_all | solution.py:192
  375.6 6.8 %copy-start.6 = (f32[320,576]{1,0:T(8,128)S(1)}, f32[320,576]{1,0:T(8,128)}, u32[]{:S(2)}) copy-start(f32[320,576]{1,0:T(8,128)} %get-tuple-element.399) | copy-start | bytes 2211844
  375.6 6.8 %copy-start.14 = (bf16[1,6144,576]{1,2,0:T(8,128)(2,1)S(1)}, bf16[1,6144,576]{1,2,0:T(8,128)(2,1)}, u32[]{:S(2)}) copy-start(bf16[1,6144,576]{1,2,0:T(8,128)(2,1)} %all-gather.11.cloned.1.call-done) | copy-start | bytes 21233668
  394.6 10.1 %copy-start.10 = (bf16[2,8,6144]{2,1,0:T(8,128)(2,1)S(1)}, bf16[2,8,6144]{2,1,0:T(8,128)(2,1)}, u32[]{:S(2)}) copy-start(bf16[2,8,6144]{2,1,0:T(8,128)(2,1)} %param.28) | copy-start | bytes 589828
  394.6 10.1 %copy-start.11 = (bf16[6144,4]{0,1:T(4,128)(2,1)S(1)}, bf16[6144,4]{0,1:T(4,128)(2,1)}, u32[]{:S(2)}) copy-start(bf16[6144,4]{0,1:T(4,128)(2,1)} %param.30) | copy-start | bytes 147460
  394.6 150.2 %all-to-all-start.2 = ((bf16[32,10,6144]{2,1,0:T(8,128)(2,1)}), bf16[32,10,6144]{2,1,0:T(8,128)(2,1)}, u32[]{:S(2)}, u32[]{:S(2)}) async-start(bf16[32,10,6144]{2,1,0:T(8,128)(2,1)} %reshape.276), calls=%async_computation.2 | async-start | bytes 12582912 | tf_op jit(solution)/shard_map/all_to_all | solution.py:191
  410.0 23.8 %copy-start.2 = (bf16[2,256,256]{1,2,0:T(8,128)(2,1)S(1)}, bf16[2,256,256]{1,2,0:T(8,128)(2,1)}, u32[]{:S(2)}) copy-start(bf16[2,256,256]{1,2,0:T(8,128)(2,1)} %copy-done.1) | copy-start | bytes 786436
  428.8 7.0 %copy-start.12 = (s32[2,8,2]{1,2,0:T(2,128)S(1)}, s32[2,8,2]{1,2,0:T(2,128)}, u32[]{:S(2)}) copy-start(s32[2,8,2]{1,2,0:T(2,128)} %param.31) | copy-start | bytes 388
Sparse Core Ops, SparseCore 0:
  12.4 29.5 all-gather.14
  43.8 46.4 all-gather.12
  92.2 46.8 all-gather.10
  140.7 46.8 all-gather.8
  214.3 28.8 all-gather.16
where the time goes:
time: 575 us; the launch traced here: 566 us
  waiting for transfers between devices  352 us (61%)
  matrix products  56.7 us (10%)
  local copies, waits for them, and re-layouts  48.1 us (8%)
  starting transfers between devices  47.9 us (8%)
  other arithmetic  23.5 us (4%)
  between operations  16.5 us (3%)
  blocking collectives  11 us (2%)
  loops' own time  10.5 us (2%)
    all_to_all x1, waiting for transfers between devices, on_device(): lax.all_to_all(spread(grad_buffer), 'expert', split_axis=0, concat_axis=0...  131 us
    all_to_all x1, waiting for transfers between devices, on_device(): lax.all_to_all(spread(token_buffer), 'expert', split_axis=0, concat_axis=...  110 us
    all_to_all x1, waiting for transfers between devices, on_device(): lax.all_to_all(slice_dx, 'expert', split_axis=0, concat_axis=0, tiled=True)  109 us
    select_n x16, other arithmetic, lap(): return jax.tree.map(lambda a, b: jnp.where(reached, a, b), new, before)  16.9 us
    all_to_all x1, starting transfers between devices, on_device(): lax.all_to_all(spread(token_buffer), 'expert', split_axis=0, concat_axis=...  14.6 us
    all_to_all x1, starting transfers between devices, on_device(): lax.all_to_all(spread(grad_buffer), 'expert', split_axis=0, concat_axis=0...  11.7 us
  transfers between devices with their start and end apart: 9, of which 3 were waited for; matrix products, arithmetic and copies ran while one was open for 19% of the time, Pallas kernels for 0%

commit v1 on v0

v1 whole, which is shorter than its diff:
```python
import jax
import jax.numpy as jnp
from jax import lax
from jax.experimental import pallas as pl
from jax.experimental.pallas import tpu as pltpu
from jax.sharding import Mesh, PartitionSpec as P

highest = lax.Precision.HIGHEST
norm_epsilon = 1e-06
MESH = pl.DeviceIdType.MESH
AXES_SEQ = ("x", "c")
AXES_EXPERT = ("z", "y")

D = 6144
W_ROWS = 768
H_MAIN = 512
H_TAIL = 64
N_IN = 1152
N_ALL = 1792
TOK = 16
CAP = 80
HALF = 3072
D_EXT = D + 128


def expert_kernel(
    tok, grd, info, wall, out,
    wbuf, zx, zg, zi, xa, ga, pre, ugr, ggu, dxs, yha, yhb, yfp, yfm, cz, zr, zl, psel,
    ssem, rsem, lsem,
):
    x, c, z, y = (lax.axis_index(a) for a in ("x", "c", "z", "y"))
    xp, xm = (x + 1) % 4, (x + 3) % 4
    yp, ym, y2 = (y + 1) % 4, (y + 3) % 4, (y + 2) % 4
    zp, zm = (z + 1) % 8, (z + 7) % 8
    right = {"x": {"x": xp}, "y": {"y": yp}, "z": {"z": zp}}
    left = {"x": {"x": xm}, "y": {"y": ym}, "z": {"z": zm}}
    sib = {"c": 1 - c}
    me = 2 * x + c
    started = []

    def send(src, dst, dev):
        at = len(started)
        copy = pltpu.make_async_remote_copy(
            src_ref=src, dst_ref=dst, send_sem=ssem.at[at], recv_sem=rsem.at[at],
            device_id=dev, device_id_type=MESH,
        )
        copy.start()
        started.append(copy)
        return copy

    barrier = pltpu.get_barrier_semaphore()
    peers = [right[a] for a in "xyz"] + [left[a] for a in "xyz"] + [sib]
    for peer in peers:
        pl.semaphore_signal(barrier, inc=1, device_id=peer, device_id_type=MESH)
    pl.semaphore_wait(barrier, len(peers))

    half_a, half_b = pl.ds(0, W_ROWS // 2), pl.ds(W_ROWS // 2, W_ROWS // 2)
    wra = send(wall.at[half_a], wbuf.at[me, half_a], right["x"])
    wlb = send(wall.at[half_b], wbuf.at[me, half_b], left["x"])
    zxr = [send(tok, zx.at[z], right["z"])]
    zxl = [send(tok, zx.at[z], left["z"])]
    zir = [send(info, zi.at[z], right["z"])]
    zil = [send(info, zi.at[z], left["z"])]
    wrb = send(wall.at[half_b], wbuf.at[me, half_b], right["x"])
    wla = send(wall.at[half_a], wbuf.at[me, half_a], left["x"])
    ws = [send(wall, wbuf.at[me], sib)]
    own = pltpu.make_async_copy(wall, wbuf.at[me], lsem.at[0])
    own.start()
    zx[z] = tok[...]
    zg[z] = grd[...]
    zi[z] = info[...]
    pre[...] = jnp.zeros_like(pre)
    ugr[...] = jnp.zeros_like(ugr)

    def z_hop(h, buf, rights, lefts):
        rights[h - 1].wait_recv()
        if h < 4:
            at = (z + 8 - h) % 8
            rights.append(send(buf.at[at], buf.at[at], right["z"]))
        if h <= 3:
            lefts[h - 1].wait_recv()
            if h < 3:
                at = (z + h) % 8
                lefts.append(send(buf.at[at], buf.at[at], left["z"]))

    for h in range(1, 5):
        z_hop(h, zx, zxr, zxl)
        z_hop(h, zi, zir, zil)
    zgr = [send(grd, zg.at[z], right["z"])]
    zgl = [send(grd, zg.at[z], left["z"])]

    k = z // 2
    total = zi[0]
    for i in range(1, 8):
        total = total + zi[i]
    kind = lax.broadcasted_iota(jnp.int32, (8, 128), 0)
    slot_row = jnp.sum(jnp.where(kind == k, total, 0.0), axis=0, keepdims=True)
    gate_row = jnp.sum(jnp.where(kind == k + 4, total, 0.0), axis=0, keepdims=True)
    rows = lax.broadcasted_iota(jnp.int32, (CAP, 128), 0).astype(jnp.float32) + 1.0
    hot = (rows == jnp.broadcast_to(slot_row, (CAP, 128))).astype(jnp.float32)
    gate_slot = jnp.sum(hot * jnp.broadcast_to(gate_row, (CAP, 128)), axis=1, keepdims=True)
    psel[...] = hot.astype(jnp.bfloat16)

    def compact(buf, dst):
        @pl.loop(0, D // 512)
        def _(i):
            cols = pl.ds(pl.multiple_of(i * 512, 512), 512)
            block = buf[:, :, cols].reshape(8 * TOK, 512)
            dst[y, :, cols] = jnp.dot(
                psel[...], block, preferred_element_type=jnp.float32
            ).astype(jnp.bfloat16)

    col_a, col_b = pl.ds(0, HALF), pl.ds(HALF, HALF)

    def y_send(buf):
        ra = send(buf.at[y, :, col_a], buf.at[y, :, col_a], right["y"])
        lb = send(buf.at[y, :, col_b], buf.at[y, :, col_b], left["y"])
        rb = send(buf.at[y, :, col_b], buf.at[y, :, col_b], right["y"])
        la = send(buf.at[y, :, col_a], buf.at[y, :, col_a], left["y"])
        return ra, lb, rb, la

    def y_relay(buf, ra, lb):
        ra.wait_recv()
        fa = send(buf.at[ym, :, col_a], buf.at[ym, :, col_a], right["y"])
        lb.wait_recv()
        fb = send(buf.at[yp, :, col_b], buf.at[yp, :, col_b], left["y"])
        return fa, fb

    compact(zx, xa)
    yx = y_send(xa)
    z_hop(1, zg, zgr, zgl)
    s_xm, s_xp, s_x2 = 2 * xm + c, 2 * xp + c, 2 * ((x + 2) % 4) + c
    wra.wait_recv()
    wfa = send(wbuf.at[s_xm, half_a], wbuf.at[s_xm, half_a], right["x"])
    ws.append(send(wbuf.at[s_xm, half_a], wbuf.at[s_xm, half_a], sib))
    wlb.wait_recv()
    wfb = send(wbuf.at[s_xp, half_b], wbuf.at[s_xp, half_b], left["x"])
    ws.append(send(wbuf.at[s_xp, half_b], wbuf.at[s_xp, half_b], sib))
    z_hop(2, zg, zgr, zgl)
    z_hop(3, zg, zgr, zgl)
    yxf = y_relay(xa, yx[0], yx[1])
    z_hop(4, zg, zgr, zgl)
    compact(zg, ga)
    yg = y_send(ga)
    yx[2].wait_recv()
    yx[3].wait_recv()
    wrb.wait_recv()
    ws.append(send(wbuf.at[s_xm, half_b], wbuf.at[s_xm, half_b], sib))
    wla.wait_recv()
    ws.append(send(wbuf.at[s_xp, half_a], wbuf.at[s_xp, half_a], sib))
    yxf[0].wait_recv()
    yxf[1].wait_recv()

    def add_in(shard):
        cols = pl.ds(pl.multiple_of(shard * W_ROWS, W_ROWS), W_ROWS)
        left_op = xa[:, :, cols].reshape(4 * CAP, W_ROWS)
        for at, wide in ((0, 256), (256, 256), (512, 256), (768, 256), (1024, 128)):
            pre[:, at : at + wide] += jnp.dot(
                left_op, wbuf[shard, :, at : at + wide], preferred_element_type=jnp.float32
            )

    def add_out(shard):
        cols = pl.ds(pl.multiple_of(shard * W_ROWS, W_ROWS), W_ROWS)
        left_op = ga[:, :, cols].reshape(4 * CAP, W_ROWS)
        for at, wide in ((0, 256), (256, 256), (512, 128)):
            ugr[:, at : at + wide] += jnp.dot(
                left_op, wbuf[shard, :, N_IN + at : N_IN + at + wide],
                preferred_element_type=jnp.float32,
            )

    own.wait()
    for copy in ws:
        copy.wait_recv()
    ws_done = len(ws)

    @pl.loop(0, 6)
    def _(i):
        add_in((2 * (x + 3) + i) % 8)

    ygf = y_relay(ga, yg[0], yg[1])
    yg[2].wait_recv()
    yg[3].wait_recv()
    ygf[0].wait_recv()
    ygf[1].wait_recv()

    @pl.loop(0, 6)
    def _(i):
        add_out((2 * (x + 3) + i) % 8)

    wfa.wait_recv()
    ws.append(send(wbuf.at[s_x2, half_a], wbuf.at[s_x2, half_a], sib))
    wfb.wait_recv()
    ws.append(send(wbuf.at[s_x2, half_b], wbuf.at[s_x2, half_b], sib))
    add_in(s_x2)
    add_out(s_x2)
    for copy in ws[ws_done:]:
        copy.wait_recv()
    s_x2o = 2 * ((x + 2) % 4) + 1 - c
    add_in(s_x2o)
    add_out(s_x2o)

    lane = lax.broadcasted_iota(jnp.int32, (TOK, 128), 1)

    def grads(gate, up, unit):
        sig = jax.nn.sigmoid(gate)
        act = gate * sig
        up_grad = unit * act
        gate_grad = unit * up * sig * (1.0 + gate * (1.0 - sig))
        score = jnp.sum(act * up * unit, axis=1, keepdims=True)
        return gate_grad, up_grad, score

    @pl.loop(0, 4)
    def _(b):
        @pl.loop(0, CAP // TOK)
        def _(i):
            at = pl.multiple_of(b * CAP + i * TOK, TOK)
            r = pl.ds(at, TOK)
            gg, ug, s1 = grads(pre[r, 0:512], pre[r, 512:1024], ugr[r, 0:512])
            tail = pre[r, 1024:1152]
            ggt, ugt, s2 = grads(tail, pltpu.roll(tail, 64, 1), ugr[r, 512:640])
            ggu[r, 0:512] = gg.astype(jnp.bfloat16)
            ggu[r, 512:1024] = ug.astype(jnp.bfloat16)
            ggu[r, 1024:1152] = (ggt + pltpu.roll(ugt, 64, 1)).astype(jnp.bfloat16)
            score = jnp.where(lane == k, jnp.broadcast_to(s1 + s2, (TOK, 128)), 0.0)
            dxs[b, pl.ds(pl.multiple_of(i * TOK, TOK), TOK), D:D_EXT] = score.astype(jnp.bfloat16)

    def to_dx(shard):
        for at in (0, 256, 512):
            cols = pl.ds(pl.multiple_of(shard * W_ROWS + at, 256), 256)
            part = lax.dot_general(
                ggu[...], wbuf[shard, at : at + 256, 0:N_IN], (((1,), (1,)), ((), ())),
                preferred_element_type=jnp.float32,
            )
            dxs[:, :, cols] = part.astype(jnp.bfloat16).reshape(4, CAP, 256)

    ext_b = pl.ds(HALF, D_EXT - HALF)

    @pl.loop(0, 4)
    def _(i):
        to_dx(i)

    ha = send(dxs.at[y2, :, col_a], yha, right["y"])
    fma = send(dxs.at[ym, :, col_a], yfp.at[:, col_a], left["y"])

    @pl.loop(4, 8)
    def _(i):
        to_dx(i)

    hb = send(dxs.at[y2, :, ext_b], yhb, left["y"])
    fpb = send(dxs.at[yp, :, ext_b], yfm.at[:, ext_b], right["y"])

    def add_rows(dst, add, lo, n):
        @pl.loop(0, n // 128)
        def _(i):
            to = pl.ds(pl.multiple_of(lo + i * 128, 128), 128)
            fr = pl.ds(pl.multiple_of(i * 128, 128), 128)
            dst[:, to] = (
                dst[:, to].astype(jnp.float32) + add[:, fr].astype(jnp.float32)
            ).astype(jnp.bfloat16)

    ha.wait_recv()
    add_rows(dxs.at[yp], yha, 0, HALF)
    fpa = send(dxs.at[yp, :, col_a], yfm.at[:, col_a], right["y"])
    hb.wait_recv()
    add_rows(dxs.at[ym], yhb, HALF, D_EXT - HALF)
    fmb = send(dxs.at[ym, :, ext_b], yfp.at[:, ext_b], left["y"])
    for copy in (fma, fpb, fpa, fmb):
        copy.wait_recv()

    def spread(cols, wide, gated):
        part = dxs[y, :, cols].astype(jnp.float32) + yfp[:, cols].astype(jnp.float32)
        part = part + yfm[:, cols].astype(jnp.float32)
        if gated:
            part = part * gate_slot
        back = lax.dot_general(
            psel[...], part.astype(jnp.bfloat16), (((0,), (0,)), ((), ())),
            preferred_element_type=jnp.float32,
        )
        cz[:, :, cols] = back.astype(jnp.bfloat16).reshape(8, TOK, wide)

    @pl.loop(0, D // 512)
    def _(i):
        spread(pl.ds(pl.multiple_of(i * 512, 512), 512), 512, True)

    spread(pl.ds(D, 128), 128, False)

    parts = (col_a, ext_b)

    def z_first(dst, dev, at):
        return [send(cz.at[at, :, p], dst.at[0, :, p], dev) for p in parts]

    zrc = [z_first(zr, right["z"], (z + 4) % 8)]
    zlc = [z_first(zl, left["z"], (z + 5) % 8)]
    for h in range(1, 4):
        nr, nl = [], []
        for n, p in enumerate(parts):
            at = (z + 4 - h) % 8
            zrc[h - 1][n].wait_recv()
            cz[at, :, p] = (
                cz[at, :, p].astype(jnp.float32) + zr[h - 1, :, p].astype(jnp.float32)
            ).astype(jnp.bfloat16)
            nr.append(send(cz.at[at, :, p], zr.at[h, :, p], right["z"]))
            if h < 3:
                at = (z + 5 + h) % 8
                zlc[h - 1][n].wait_recv()
                cz[at, :, p] = (
                    cz[at, :, p].astype(jnp.float32) + zl[h - 1, :, p].astype(jnp.float32)
                ).astype(jnp.bfloat16)
                nl.append(send(cz.at[at, :, p], zl.at[h, :, p], left["z"]))
        zrc.append(nr)
        zlc.append(nl)
    for n, p in enumerate(parts):
        zlc[2][n].wait_recv()
        zrc[3][n].wait_recv()
        out[:, p] = (
            cz[z, :, p].astype(jnp.float32)
            + zr[3, :, p].astype(jnp.float32)
            + zl[2, :, p].astype(jnp.float32)
        )
    for copy in started:
        copy.wait_send()


def expert_block(tok, grd, info, wall):
    bf16, f32 = jnp.bfloat16, jnp.float32
    vmem = pl.BlockSpec(memory_space=pltpu.VMEM)
    n_copies = 66
    return pl.pallas_call(
        expert_kernel,
        out_shape=jax.ShapeDtypeStruct((TOK, D_EXT), f32),
        in_specs=[vmem, vmem, vmem, pl.BlockSpec(memory_space=pl.ANY)],
        out_specs=vmem,
        scratch_shapes=[
            pltpu.VMEM((8, W_ROWS, N_ALL), bf16),
            pltpu.VMEM((8, TOK, D), bf16),
            pltpu.VMEM((8, TOK, D), bf16),
            pltpu.VMEM((8, 8, 128), f32),
            pltpu.VMEM((4, CAP, D), bf16),
            pltpu.VMEM((4, CAP, D), bf16),
            pltpu.VMEM((4 * CAP, N_IN), f32),
            pltpu.VMEM((4 * CAP, N_ALL - N_IN), f32),
            pltpu.VMEM((4 * CAP, N_IN), bf16),
            pltpu.VMEM((4, CAP, D_EXT), bf16),
            pltpu.VMEM((CAP, HALF), bf16),
            pltpu.VMEM((CAP, D_EXT - HALF), bf16),
            pltpu.VMEM((CAP, D_EXT), bf16),
            pltpu.VMEM((CAP, D_EXT), bf16),
            pltpu.VMEM((8, TOK, D_EXT), bf16),
            pltpu.VMEM((4, TOK, D_EXT), bf16),
            pltpu.VMEM((3, TOK, D_EXT), bf16),
            pltpu.VMEM((CAP, 128), bf16),
            pltpu.SemaphoreType.DMA((n_copies,)),
            pltpu.SemaphoreType.DMA((n_copies,)),
            pltpu.SemaphoreType.DMA((1,)),
        ],
        compiler_params=pltpu.CompilerParams(
            collective_id=0, has_side_effects=True, vmem_limit_bytes=64 * 1024 * 1024 - 65536
        ),
        cost_estimate=pl.CostEstimate(
            flops=12 * 10**9, bytes_accessed=40 * 10**6, transcendentals=200000
        ),
        name="expert_block",
    )(tok, grd, info, wall)


def entering(x, axis, combine, identity, reverse):
    length, here = (8, 2 * lax.axis_index("x") + lax.axis_index("c"))
    everything = jax.tree.map(lambda part: lax.all_gather(part, axis), x)
    start = jax.tree.map(
        lambda part, zero: jnp.broadcast_to(jnp.asarray(zero, part.dtype), part.shape), x, identity
    )

    def lap(k, before):
        at = length - 1 - k if reverse else k
        reached = at > here if reverse else at < here
        new = combine(before, jax.tree.map(lambda part: part[at], everything))
        return jax.tree.map(lambda a, b: jnp.where(reached, a, b), new, before)

    return lax.fori_loop(0, length, lap, start)


def carry_combine(earlier, later):
    return (earlier[0] * later[0], later[0] * earlier[1] + later[1])


def earlier_state(summary, block_decay):
    identity = (jnp.ones_like(block_decay), jnp.zeros_like(summary))
    result = entering((block_decay, summary), AXES_SEQ, carry_combine, identity, False)
    return result[1]


def later_state(summary, block_decay):
    identity = (jnp.ones_like(block_decay), jnp.zeros_like(summary))
    result = entering((block_decay, summary), AXES_SEQ, carry_combine, identity, True)
    return result[1]


def on_device(
    queries,
    key_rows,
    value_rows,
    decay_rate,
    norm_gain,
    attn_probe,
    hidden_in,
    moe_probe,
    router_weight,
    routes,
    gate_weight,
    up_weight,
    down_weight,
    rollout_logprob,
    trainer_logprob,
    advantage,
    clip_low,
    clip_high,
):
    rollouts, block_size, feature_width = queries.shape
    head_count = decay_rate.shape[0]
    head_size = feature_width // head_count
    importance = jnp.exp(trainer_logprob - rollout_logprob)
    clipped = jnp.minimum(jnp.maximum(importance, clip_low[0]), clip_high[0])
    coeff = -(clipped * advantage) / rollouts
    objective = coeff * trainer_logprob
    shape_four = (rollouts, block_size, head_count, head_size)
    query_full = queries.reshape(shape_four).astype(jnp.float32)
    key_full = key_rows.reshape(shape_four).astype(jnp.float32)
    value_full = value_rows.reshape(shape_four).astype(jnp.float32)
    probe_full = attn_probe.reshape(shape_four).astype(jnp.float32)
    gain_full = norm_gain.reshape(head_count, head_size)
    offsets = jnp.arange(block_size, dtype=jnp.float32)
    rate_row = decay_rate[None, :]
    distance = offsets[:, None] - offsets[None, :]
    within = jnp.where(
        (distance >= 0)[None],
        jnp.exp(-decay_rate[:, None, None] * jnp.maximum(distance, 0.0)[None]),
        0.0,
    )
    lead_decay = jnp.exp(-rate_row * (offsets[:, None] + 1.0))[None, :, :, None]
    key_tail = jnp.exp(-rate_row * (block_size - 1.0 - offsets[:, None]))[None, :, :, None]
    query_tail = jnp.exp(-rate_row * offsets[:, None])[None, :, :, None]
    grad_tail = jnp.exp(-rate_row * (block_size - offsets[:, None]))[None, :, :, None]
    block_decay = jnp.exp(-decay_rate * block_size).reshape(1, head_count, 1, 1)
    forward_summary = jnp.einsum(
        "rjhk,rjhv->rhkv", key_full * key_tail, value_full, precision=highest
    )
    state_before = earlier_state(forward_summary, block_decay)
    scores = jnp.einsum("rihc,rjhc->rhij", query_full, key_full, precision=highest) * within[None]
    output = jnp.einsum("rhij,rjhv->rihv", scores, value_full, precision=highest)
    output = output + lead_decay * jnp.einsum(
        "rihk,rhkv->rihv", query_full, state_before, precision=highest
    )
    inverse = lax.rsqrt(jnp.mean(output * output, axis=-1, keepdims=True) + norm_epsilon)
    scaled = gain_full[None, None] * (coeff[:, :, None, None] * probe_full)
    grad_out = inverse * scaled - output * inverse**3 * jnp.mean(
        scaled * output, axis=-1, keepdims=True
    )
    backward_summary = jnp.einsum(
        "rihk,rihv->rhkv", query_full * query_tail, grad_out, precision=highest
    )
    state_after = later_state(backward_summary, block_decay)
    product = jnp.einsum("rihv,rjhv->rhij", grad_out, value_full, precision=highest) * within[None]
    grad_query = jnp.einsum("rhij,rjhk->rihk", product, key_full, precision=highest)
    grad_query = grad_query + lead_decay * jnp.einsum(
        "rihv,rhkv->rihk", grad_out, state_before, precision=highest
    )
    grad_key = jnp.einsum("rhij,rihk->rjhk", product, query_full, precision=highest)
    grad_key = grad_key + grad_tail * jnp.einsum(
        "rjhv,rhkv->rjhk", value_full, state_after, precision=highest
    )
    grad_value = jnp.einsum("rhij,rihv->rjhv", scores, grad_out, precision=highest)
    grad_value = grad_value + grad_tail * jnp.einsum(
        "rjhk,rhkv->rjhv", key_full, state_after, precision=highest
    )
    out_shape = (rollouts, block_size, feature_width)
    grad_queries = grad_query.reshape(out_shape).astype(jnp.bfloat16)
    grad_keys = grad_key.reshape(out_shape).astype(jnp.bfloat16)
    grad_values = grad_value.reshape(out_shape).astype(jnp.bfloat16)
    positions, model_width = hidden_in.shape[1:]
    experts = router_weight.shape[1]
    z_index = lax.axis_index("z")
    local_coeff = lax.dynamic_slice_in_dim(
        coeff, (4 * z_index + lax.axis_index("y")) * positions, positions, 1
    )
    grad_rows = (local_coeff[:, :, None] * moe_probe.astype(jnp.float32)).astype(jnp.bfloat16)
    onehot = (routes[..., None] == jnp.arange(experts, dtype=jnp.int32)).astype(jnp.float32)
    member = onehot.sum(axis=2)
    rank = jnp.cumsum(member, axis=1) - member
    slot = rank + 5.0 * jnp.arange(rollouts, dtype=jnp.float32)[:, None, None]
    slot = jnp.where(member > 0, slot + 1.0 + (10 * z_index).astype(jnp.float32), 0.0)
    logits = jnp.einsum("rpd,de->rpe", hidden_in, router_weight, preferred_element_type=jnp.float32)
    chosen = jnp.einsum("rpke,rpe->rpk", onehot, logits, precision=highest)
    exponent = jnp.exp(chosen)
    gates = exponent / jnp.sum(exponent, axis=-1, keepdims=True)
    gate_expert = jnp.einsum("rpk,rpke->rpe", gates, onehot, precision=highest)
    both = jnp.concatenate([slot, gate_expert], axis=2).reshape(TOK, 2 * experts).T
    info = lax.dynamic_update_slice(
        jnp.zeros((2 * experts, 128), jnp.float32), both, (0, TOK * z_index)
    )
    gate, up, down = gate_weight[0], up_weight[0], down_weight[0]
    wall = jnp.concatenate(
        [
            gate[:, :H_MAIN], up[:, :H_MAIN], gate[:, H_MAIN:], up[:, H_MAIN:],
            down, jnp.zeros((W_ROWS, H_TAIL), jnp.bfloat16),
        ],
        axis=1,
    )
    summed = expert_block(
        hidden_in.reshape(TOK, model_width), grad_rows.reshape(TOK, model_width), info, wall
    )
    row_score = summed[:, model_width : model_width + experts].reshape(rollouts, positions, experts)
    score_pick = jnp.einsum("rpke,rpe->rpk", onehot, row_score, precision=highest)
    score_mean = jnp.sum(gates * score_pick, axis=-1, keepdims=True)
    logit_grad = gates * (score_pick - score_mean)
    logit_expert = jnp.einsum("rpk,rpke->rpe", logit_grad, onehot, precision=highest)
    grad_hidden = summed[:, :model_width].reshape(rollouts, positions, model_width)
    grad_hidden = grad_hidden + jnp.einsum(
        "rpe,de->rpd", logit_expert, router_weight.astype(jnp.float32), precision=highest
    )
    return (objective, grad_queries, grad_keys, grad_values, grad_hidden.astype(jnp.bfloat16))


def solution(mesh):
    grid = Mesh(mesh.devices.reshape(4, 2, 8, 4), ("x", "c", "z", "y"))
    seq, exp = AXES_SEQ, AXES_EXPERT
    rows = P(None, seq, exp)
    toks = P(None, seq + exp, None)
    wts = P(exp, seq, None)
    in_specs = (
        rows, rows, rows, P(exp), P(exp), rows, toks, toks, P(), toks, wts, wts, wts,
        P(None, seq), P(None, seq), P(None, seq), P(), P(),
    )
    out_specs = (P(None, seq), rows, rows, rows, toks)
    return jax.shard_map(
        on_device, mesh=grid, in_specs=in_specs, out_specs=out_specs, check_vma=False
    )
```

time: 575 us -> 275 us (0.48); the launches traced: 566 us -> 272 us
  waiting for transfers between devices: 352 us -> 0.58 us
  Pallas kernels: 0 us -> 181 us
  starting transfers between devices: 47.9 us -> 0.08 us
  matrix products: 56.7 us -> 12.8 us
  local copies, waits for them, and re-layouts: 48.1 us -> 26.2 us
  loops' own time: 10.5 us -> 0.44 us
    all_to_all x4 -> x0, waiting for transfers between devices: 350 us -> none  [the longest x1 131 us: on_device(): lax.all_to_all(spread(grad_buffer), 'expert', split_axis=0, concat_axis=0...]
    pallas_call x0 -> x1, Pallas kernels: none -> 181 us  [expert_block(): pl.pallas_call(expert_kernel, out_shape=jax.ShapeDtypeStruct((TOK, D_EXT)...]
    all_to_all x4 -> x0, starting transfers between devices: 47.7 us -> none  [the longest x1 14.6 us: on_device(): lax.all_to_all(spread(token_buffer), 'expert', split_axis=0, concat_axis=...]
    dot_general x10 -> x0, matrix products: 43.3 us -> none  [the longest x1 8.44 us: on_device(): unit_grad = jnp.dot(grad_flat, down_mat, preferred_element_type=jnp.float32)]
    reshape x5 -> x2, local copies, waits for them, and re-layouts: 32.6 us -> 0.88 us  [the longest x1 0.8 us: on_device(): summed[:, model_width:model_width + experts]]
    another operation x2, loops' own time: 10.5 us -> 0.44 us  [entering(): return lax.fori_loop(0, length, lap, start)]
  transfers between devices with their start and end apart: 9 -> 2, of which waited for: 3 -> 1; matrix products, arithmetic and copies ran while one was open for 19% -> 9% of each run, Pallas kernels for 0% -> 66%
where the time goes in v1:
time: 275 us; the launch traced here: 272 us
  Pallas kernels  181 us (66%)
  local copies, waits for them, and re-layouts  26.2 us (10%)
  other arithmetic  23.4 us (9%)
  between operations  16.6 us (6%)
  matrix products  12.8 us (5%)
  blocking collectives  11.3 us (4%)
    pallas_call x1, Pallas kernels, expert_block(): pl.pallas_call(expert_kernel, out_shape=jax.ShapeDtypeStruct((TOK, D_EXT)...  181 us
    select_n x16, other arithmetic, lap(): return jax.tree.map(lambda a, b: jnp.where(reached, a, b), new, before)  16.8 us
    unnamed x1, blocking collectives  11.3 us
    unnamed x79, local copies, waits for them, and re-layouts  9.39 us
  transfers between devices with their start and end apart: 2, of which 1 were waited for; matrix products, arithmetic and copies ran while one was open for 9% of the time, Pallas kernels for 66%

profile of v1, /device:TPU:6, one launch (start us, length us, event | category | flops | bytes accessed | tf_op | source)
XLA Modules:
  0.0 272.4 jit_solution(4163557952526147381)
XLA Ops:
  7.3 1.1 copy.196
  8.4 1.3 dynamic-slice
  10.4 0.7 fusion.42
  11.8 2.0 fusion.17
  14.7 0.7 slice.26
  16.0 1.0 slice.25
  17.0 0.7 slice.27
  20.8 1.5 copy.130
  22.3 11.3 %all-reduce = f32[16]{0:T(128)S(1)} all-reduce(f32[16]{0:T(128)S(1)} %get-tuple-element.362), channel_id=2, replica_groups=mesh['x'=4,'c'=2,'z'=8,'y'=4] {'x','c'}, use_global_device_ids=true, to_apply=%add | all-reduce | flops 16 | bytes 128
  33.9 1.2 copy.115
  35.3 0.7 broadcast_in_dim.20
  36.1 4.9 %concatenate.7.wall = bf16[768,1792]{1,0:T(8,128)(2,1)} concatenate(bf16[768,512]{1,0:T(8,128)(2,1)S(1)} %slice.24, bf16[768,512]{1,0:T(8,128)(2,1)} %slice.25, bf16[768,64]{1,0:T(8,128)(2,1)S(1)} %copy-done.18, bf16[768,64]{1,0:T(8,128)(2,1)S(1)} %copy-done.19, bf16[768,576]{1,0:T(8,128)(2,1)S(1)} %bitcast.163, bf16[768,64]{1,0:T(8,128)(2,1)} %broadcast_in_dim.20), dimensions={1} | concatenate | bytes 5505024 | tf_op jit(solution)/shard_map/concatenate | solution.py:501
  41.9 0.8 copy-done.8
  43.6 8.7 %while.30 = (s32[]{:T(128)}, f32[2,2,128,128]{3,2,1,0:T(8,128)S(1)}, s32[]{:T(128)}, f32[8,1,2,1,1]{2,4,3,1,0:T(1,128)S(1)}, f32[8,2,2,128,128]{4,3,2,1,0:T(8,128)}, /*index=5*/s32[]{:T(128)}, s32[]{:T(128)}) while((s32[]{:T(128)}, f32[2,2,128,128]{3,2,1,0:T(8,128)S(1)}, s32[]{:T(128)}, f32[8,1,2,1,1]{2,4,3,1,0:T(1,128)S(1)}, ...), condition=%wide.region_1.2_spmd.clone, body=%wide.region_0.1_spmd.clone.sunk | while | flops 262148 | bytes 786561 | solution.py:379
  43.6 1.1 fusion.69
  44.8 1.1 fusion.69
  45.9 1.1 fusion.69
  47.0 1.1 fusion.69
  48.0 1.1 fusion.69
  49.1 1.1 fusion.69
  50.2 1.1 fusion.69
  51.3 1.1 fusion.69
  52.9 0.8 multiply_reduce_fusion.1
  53.9 0.8 copy-done
  54.7 1.4 fusion.14
  56.1 0.8 fusion.32.grd
  56.9 181.0 %expert_block.1 = f32[16,6272]{1,0:T(8,128)} custom-call(bf16[16,6144]{1,0:T(8,128)(2,1)} %bitcast.175, bf16[16,6144]{1,0:T(8,128)(2,1)} %fusion.32.grd, f32[8,128]{1,0:T(8,128)} %copy-done.29, bf16[768,1792]{1,0:T(8,128)(2,1)} %concatenate.7.wall), custom_call_target="tpu_custom_call" | custom-call | flops 12000000000 | bytes 40000000 | tf_op jit(solution)/shard_map/expert_block/pallas_call | solution.py:328
  237.9 0.8 slice_bitcast_fusion
  238.8 0.7 select_reduce_fusion.1
  239.5 0.7 multiply_reduce_fusion.2
  240.9 0.7 select_reduce_fusion
  241.6 2.1 fusion.2
  243.7 1.7 fusion.10
  246.1 0.7 fusion.11
  246.8 0.8 copy.132
  247.6 13.7 %while.31 = (s32[]{:T(128)}, f32[2,2,128,128]{3,2,1,0:T(8,128)S(1)}, s32[]{:T(128)}, f32[8,1,2,1,1]{2,4,3,1,0:T(1,128)}, f32[8,2,2,128,128]{4,3,2,1,0:T(8,128)},...) while((s32[]{:T(128)}, f32[2,2,128,128]{3,2,1,0:T(8,128)S(1)}, s32[]{:T(128)}, ...), condition=%wide.region_5.6_spmd.clone, body=%wide.region_4.5_spmd.clone.sunk | while | flops 262152 | bytes 786623 | solution.py:379
  247.7 0.7 dynamic-slice_bitcast_fusion.5
  248.4 1.0 fusion.70
  250.1 1.0 fusion.70
  251.7 1.0 fusion.70
  253.4 1.0 fusion.70
  255.2 1.0 fusion.70
  256.9 1.0 fusion.70
  258.7 1.0 fusion.70
  260.3 1.0 fusion.70
  262.6 0.8 fusion.13
  263.4 0.8 copy.134
  264.7 0.8 copy.133
  (129 shorter events, 14.4 us)
Async XLA Ops:
  7.2 6.8 %copy-start.16 = (bf16[1,768,576]{1,2,0:T(8,128)(2,1)S(1)}, bf16[1,768,576]{1,2,0:T(8,128)(2,1)}, u32[]{:S(2)}) copy-start(bf16[1,768,576]{1,2,0:T(8,128)(2,1)} %param.32) | copy-start | bytes 2654212
  7.2 36.5 %all-gather.6.cloned.1.call-start = ((), (), s32[]{:S(2)}) async-start(), calls=%async_computation | async-start | bytes 2359296 | tf_op jit(solution)/shard_map/all_gather | solution.py:368
  8.4 6.3 %copy-start.12 = (bf16[2,256,256]{1,2,0:T(8,128)(2,1)}, bf16[2,256,256]{1,2,0:T(8,128)(2,1)S(1)}, u32[]{:S(2)}) copy-start(bf16[2,256,256]{1,2,0:T(8,128)(2,1)S(1)} %copy.196) | copy-start | bytes 786436
  11.8 40.6 %copy-start.26 = (f32[256,2]{0,1:T(2,128)}, f32[256,2]{0,1:T(2,128)S(1)}, u32[]{:S(2)}) copy-start(f32[256,2]{0,1:T(2,128)S(1)} %get-tuple-element.360) | copy-start | bytes 6148
  13.9 1.5 copy-start.17
  13.9 233.7 %all-gather.8.cloned.1.call-start = ((), (), s32[]{:S(2)}) async-start(), calls=%async_computation.1 | async-start | bytes 2359296 | tf_op jit(solution)/shard_map/all_gather | solution.py:368
  14.7 3.0 %copy-start.23 = (bf16[6144,4]{0,1:T(4,128)(2,1)S(1)}, bf16[6144,4]{0,1:T(4,128)(2,1)}, u32[]{:S(2)}) copy-start(bf16[6144,4]{0,1:T(4,128)(2,1)} %param.30) | copy-start | bytes 147460
  14.7 3.0 %copy-start.34 = (bf16[2,8,6144]{2,1,0:T(8,128)(2,1)S(1)}, bf16[2,8,6144]{2,1,0:T(8,128)(2,1)}, u32[]{:S(2)}) copy-start(bf16[2,8,6144]{2,1,0:T(8,128)(2,1)} %param.28) | copy-start | bytes 589828
  15.4 2.9 %copy-start.24 = (s32[2,8,2]{1,2,0:T(2,128)S(1)}, s32[2,8,2]{1,2,0:T(2,128)}, u32[]{:S(2)}) copy-start(s32[2,8,2]{1,2,0:T(2,128)} %param.31) | copy-start | bytes 388
  16.0 17.7 %copy-start.20 = (bf16[2,256,256]{2,1,0:T(8,128)(2,1)S(1)}, bf16[2,256,256]{2,1,0:T(8,128)(2,1)}, u32[]{:S(2)}) copy-start(bf16[2,256,256]{2,1,0:T(8,128)(2,1)} %param.22) | copy-start | bytes 786436
  17.7 18.4 %copy-start.18 = (bf16[768,64]{1,0:T(8,128)(2,1)S(1)}, bf16[768,64]{1,0:T(8,128)(2,1)}, u32[]{:S(2)}) copy-start(bf16[768,64]{1,0:T(8,128)(2,1)} %slice.26) | copy-start | bytes 294916
  17.7 18.4 %copy-start.19 = (bf16[768,64]{1,0:T(8,128)(2,1)S(1)}, bf16[768,64]{1,0:T(8,128)(2,1)}, u32[]{:S(2)}) copy-start(bf16[768,64]{1,0:T(8,128)(2,1)} %slice.27) | copy-start | bytes 294916
  18.3 15.4 %copy-start.22 = (f32[2,8,2]{1,2,0:T(2,128)}, f32[2,8,2]{1,2,0:T(2,128)S(1)}, u32[]{:S(2)}) copy-start(f32[2,8,2]{1,2,0:T(2,128)S(1)} %select_reduce_fusion.3) | copy-start | bytes 388
  18.3 0.6 copy-start.27
  33.9 20.0 %copy-start.6 = (bf16[2,256,256]{1,2,0:T(8,128)(2,1)}, bf16[2,256,256]{1,2,0:T(8,128)(2,1)S(1)}, u32[]{:S(2)}) copy-start(bf16[2,256,256]{1,2,0:T(8,128)(2,1)S(1)} %copy.169) | copy-start | bytes 786436
  35.3 5.6 %copy-start.29 = (f32[8,128]{1,0:T(8,128)}, f32[8,128]{1,0:T(8,128)S(1)}, u32[]{:S(2)}) copy-start(f32[8,128]{1,0:T(8,128)S(1)} %dynamic_update_slice.3.info) | copy-start | bytes 12292
  36.0 4.9 %copy-start.31 = (f32[2,256]{1,0:T(2,128)S(1)}, f32[2,256]{1,0:T(2,128)}, u32[]{:S(2)}) copy-start(f32[2,256]{1,0:T(2,128)} %param.36) | copy-start | bytes 6148
  36.0 4.9 %copy-start.32 = (f32[2,256]{1,0:T(2,128)S(1)}, f32[2,256]{1,0:T(2,128)}, u32[]{:S(2)}) copy-start(f32[2,256]{1,0:T(2,128)} %param.37) | copy-start | bytes 6148
  36.1 4.9 %copy-start.33 = (f32[2,256]{1,0:T(2,128)S(1)}, f32[2,256]{1,0:T(2,128)}, u32[]{:S(2)}) copy-start(f32[2,256]{1,0:T(2,128)} %param.35) | copy-start | bytes 6148
  36.1 6.7 %copy-start.14 = (bf16[2,256,256]{2,1,0:T(8,128)(2,1)S(1)}, bf16[2,256,256]{2,1,0:T(8,128)(2,1)}, u32[]{:S(2)}) copy-start(bf16[2,256,256]{2,1,0:T(8,128)(2,1)} %param.23) | copy-start | bytes 786436
  41.9 0.8 copy-start.8
  43.1 9.8 %copy-start.4 = (f32[2,2,256,256]{3,2,1,0:T(8,128)}, f32[2,2,256,256]{3,2,1,0:T(8,128)S(1)}, u32[]{:S(2)}) copy-start(f32[2,2,256,256]{3,2,1,0:T(8,128)S(1)} %convolution_multiply_fusion.1) | copy-start | bytes 3145732
  43.6 9.2 %copy-start.10 = (bf16[2,256,256]{2,1,0:T(8,128)(2,1)S(1)}, bf16[2,256,256]{2,1,0:T(8,128)(2,1)}, u32[]{:S(2)}) copy-start(bf16[2,256,256]{2,1,0:T(8,128)(2,1)} %param.24) | copy-start | bytes 786436
  43.6 9.2 %copy-start.30 = (f32[256]{0:T(256)S(1)}, f32[256]{0:T(256)}, u32[]{:S(2)}) copy-start(f32[256]{0:T(256)} %param.26) | copy-start | bytes 3076
  52.4 1.5 copy-start.2
  52.4 1.5 copy-start.28
  53.7 2.5 copy-start.21
  53.9 0.8 copy-start
  237.9 7.5 %copy-start.1 = (f32[2,256,2,128]{1,3,2,0:T(8,128)S(1)}, f32[2,256,2,128]{1,3,2,0:T(8,128)}, u32[]{:S(2)}) copy-start(f32[2,256,2,128]{1,3,2,0:T(8,128)} %copy-done) | copy-start | bytes 1572868
  237.9 7.5 %copy-start.9 = (f32[2,256,256]{2,1,0:T(8,128)S(1)}, f32[2,256,256]{2,1,0:T(8,128)}, u32[]{:S(2)}) copy-start(f32[2,256,256]{2,1,0:T(8,128)} %copy-done.8) | copy-start | bytes 1572868
  237.9 7.5 %copy-start.11 = (bf16[2,256,256]{2,1,0:T(8,128)(2,1)S(1)}, bf16[2,256,256]{2,1,0:T(8,128)(2,1)}, u32[]{:S(2)}) copy-start(bf16[2,256,256]{2,1,0:T(8,128)(2,1)} %param.24) | copy-start | bytes 786436
  241.6 4.5 %copy-start.13 = (bf16[2,256,256]{1,2,0:T(8,128)(2,1)S(1)}, bf16[2,256,256]{1,2,0:T(8,128)(2,1)}, u32[]{:S(2)}) copy-start(bf16[2,256,256]{1,2,0:T(8,128)(2,1)} %copy-done.12) | copy-start | bytes 786436
  245.4 2.2 copy-start.3
  247.6 13.8 %copy-start.15 = (bf16[2,256,256]{2,1,0:T(8,128)(2,1)S(1)}, bf16[2,256,256]{2,1,0:T(8,128)(2,1)}, u32[]{:S(2)}) copy-start(bf16[2,256,256]{2,1,0:T(8,128)(2,1)} %param.23) | copy-start | bytes 786436
  247.6 13.8 %copy-start.25 = (f32[256,2]{0,1:T(2,128)S(1)}, f32[256,2]{0,1:T(2,128)}, u32[]{:S(2)}) copy-start(f32[256,2]{0,1:T(2,128)} %get-tuple-element.357) | copy-start | bytes 6148
  261.4 1.2 copy-start.5
  261.8 2.4 copy-start.7
Sparse Core Ops, SparseCore 0:
  14.0 29.5 all-gather.5
  56.2 36.5 all-gather.7

commit v2 on v1

--- a/solution.py
+++ b/solution.py
@@ -20,13 +20,16 @@
 TOK = 16
 CAP = 80
 HALF = 3072
+BLOCK, HEAD = 256, 128
 D_EXT = D + 128
 
 
-def expert_kernel(
-    tok, grd, info, wall, out,
+def kernel(
+    tok, grd, info, wall, qr, kr, vr, pr, rate, gain, coef,
+    out, gq, gk, gv,
     wbuf, zx, zg, zi, xa, ga, pre, ugr, ggu, dxs, yha, yhb, yfp, yfm, cz, zr, zl, psel,
-    ssem, rsem, lsem,
+    f_own, f_sib, f_chip, b_own, b_sib, b_chip, f_far, b_far, state, dk_part, dv_part,
+    ssem, rsem, lsem, xss, xrs,
 ):
     x, c, z, y = (lax.axis_index(a) for a in ("x", "c", "z", "y"))
     xp, xm = (x + 1) % 4, (x + 3) % 4
@@ -50,6 +53,8 @@
 
     barrier = pltpu.get_barrier_semaphore()
     peers = [right[a] for a in "xyz"] + [left[a] for a in "xyz"] + [sib]
+    peers += [{"x": xp, "c": 1 - c}, {"x": xm, "c": 1 - c}, {"x": (x + 2) % 4}]
+    peers += [{"x": (x + 2) % 4, "c": 1 - c}]
     for peer in peers:
         pl.semaphore_signal(barrier, inc=1, device_id=peer, device_id_type=MESH)
     pl.semaphore_wait(barrier, len(peers))
@@ -72,6 +77,132 @@
     pre[...] = jnp.zeros_like(pre)
     ugr[...] = jnp.zeros_like(ugr)
 
+    f32, bf16 = jnp.float32, jnp.bfloat16
+    nn, nt, tn = (((1,), (0,)), ((), ())), (((1,), (1,)), ((), ())), (((0,), (0,)), ((), ()))
+
+    def mm(a, b, dims):
+        return lax.dot_general(a, b, dims, preferred_element_type=f32)
+
+    def parts_of(v):
+        high = v.astype(bf16)
+        return high, (v - high.astype(f32)).astype(bf16)
+
+    def row_decay(h, sign, shift):
+        row = lax.broadcasted_iota(jnp.int32, (BLOCK, HEAD), 0).astype(f32)
+        return jnp.exp(-rate[h] * (sign * row + shift))
+
+    def lanes(h):
+        return pl.ds(pl.multiple_of(h * HEAD, HEAD), HEAD)
+
+    def block_decay(h, blocks):
+        return jnp.exp(jnp.full((HEAD, HEAD), -rate[h] * (BLOCK * blocks), f32))
+
+    def summaries():
+        @pl.loop(0, 4)
+        def _(i):
+            r, h = i // 2, i % 2
+            v_high, v_low = parts_of(vr[r, :, lanes(h)].astype(f32) * row_decay(h, -1.0, BLOCK - 1.0))
+            key = kr[r, :, lanes(h)]
+            f_own[r, h] = mm(key, v_high, tn) + mm(key, v_low, tn)
+
+    def chip_state(own_ref, sib_ref, chip_ref, near_is_own):
+        for h in range(2):
+            mine, other = own_ref[c, h], sib_ref[c, h]
+            near = jnp.where(near_is_own, mine, other)
+            far = jnp.where(near_is_own, other, mine)
+            chip_ref[h] = near + block_decay(h, 1) * far
+
+    def far_copy(chip_ref, far_ref, base, dx, cc, to):
+        return pltpu.make_async_remote_copy(
+            src_ref=chip_ref, dst_ref=far_ref.at[dx - 1, c],
+            send_sem=xss.at[base + 2 * (dx - 1) + cc], recv_sem=xrs.at[base + 2 * (dx - 1) + c],
+            device_id={"x": to, "c": cc}, device_id_type=MESH,
+        )
+
+    def far_send(chip_ref, far_ref, base, step, finish=False):
+        for dx in (1, 2, 3):
+            to = x + step * dx
+
+            @pl.when(jnp.logical_and(to >= 0, to < 4))
+            def _():
+                for cc in (0, 1):
+                    copy = far_copy(chip_ref, far_ref, base, dx, cc, to)
+                    if finish:
+                        copy.wait_send()
+                    else:
+                        copy.start()
+
+    def far_state(chip_ref, far_ref, sib_ref, base, step, with_sib):
+        for dx in (1, 2, 3):
+            at = x - step * dx
+            there = jnp.logical_and(at >= 0, at < 4)
+
+            @pl.when(there)
+            def _():
+                for r in (0, 1):
+                    pltpu.make_async_remote_copy(
+                        src_ref=chip_ref, dst_ref=far_ref.at[dx - 1, r],
+                        send_sem=xss.at[base + 2 * (dx - 1) + r],
+                        recv_sem=xrs.at[base + 2 * (dx - 1) + r],
+                        device_id={"x": (x + 1) % 4, "c": r}, device_id_type=MESH,
+                    ).wait_recv()
+
+            @pl.when(jnp.logical_not(there))
+            def _():
+                far_ref[dx - 1] = jnp.zeros_like(far_ref[dx - 1])
+
+        for r in range(2):
+            for h in range(2):
+                two = block_decay(h, 2)
+                far = far_ref[0, r, h] + two * (far_ref[1, r, h] + two * far_ref[2, r, h])
+                near = sib_ref[r, h] + block_decay(h, 1) * far
+                state[r, h] = jnp.where(with_sib, near, far)
+
+    def attention_main():
+        @pl.loop(0, 4)
+        def _(i):
+            r, h = i // 2, i % 2
+            query, key, value = qr[r, :, lanes(h)], kr[r, :, lanes(h)], vr[r, :, lanes(h)]
+            at_i = lax.broadcasted_iota(jnp.int32, (BLOCK, BLOCK), 0)
+            at_j = lax.broadcasted_iota(jnp.int32, (BLOCK, BLOCK), 1)
+            apart = jnp.maximum(at_i - at_j, 0).astype(f32)
+            within = jnp.where(at_i >= at_j, jnp.exp(-rate[h] * apart), 0.0)
+            s_high, s_low = parts_of(mm(query, key, nt) * within)
+            t_high, t_low = parts_of(state[r, h])
+            lead = row_decay(h, 1.0, 1.0)
+            attn = mm(s_high, value, nn) + mm(s_low, value, nn)
+            attn = attn + lead * (mm(query, t_high, nn) + mm(query, t_low, nn))
+            inverse = lax.rsqrt(jnp.mean(attn * attn, axis=1, keepdims=True) + norm_epsilon)
+            scaled = gain[:, lanes(h)] * (coef[r] * pr[r, :, lanes(h)].astype(f32))
+            along = jnp.mean(scaled * attn, axis=1, keepdims=True)
+            grad = inverse * scaled - attn * (inverse * inverse * inverse * along)
+            g_high, g_low = parts_of(grad)
+            d_high, d_low = parts_of(grad * row_decay(h, 1.0, 0.0))
+            b_own[r, h] = mm(query, d_high, tn) + mm(query, d_low, tn)
+            p_high, p_low = parts_of((mm(g_high, value, nt) + mm(g_low, value, nt)) * within)
+            dq = mm(p_high, key, nn) + mm(p_low, key, nn)
+            dq = dq + lead * (mm(g_high, t_high, nt) + mm(g_low, t_high, nt) + mm(g_high, t_low, nt))
+            gq[r, :, lanes(h)] = dq.astype(bf16)
+            dk_part[r, :, lanes(h)] = mm(p_high, query, tn) + mm(p_low, query, tn)
+            dv_part[r, :, lanes(h)] = (
+                mm(s_high, g_high, tn) + mm(s_low, g_high, tn) + mm(s_high, g_low, tn)
+            )
+
+    def attention_last():
+        @pl.loop(0, 4)
+        def _(i):
+            r, h = i // 2, i % 2
+            key, value = kr[r, :, lanes(h)], vr[r, :, lanes(h)]
+            t_high, t_low = parts_of(state[r, h])
+            tail = row_decay(h, -1.0, float(BLOCK))
+            dk = dk_part[r, :, lanes(h)] + tail * (mm(value, t_high, nt) + mm(value, t_low, nt))
+            dv = dv_part[r, :, lanes(h)] + tail * (mm(key, t_high, nn) + mm(key, t_low, nn))
+            gk[r, :, lanes(h)] = dk.astype(bf16)
+            gv[r, :, lanes(h)] = dv.astype(bf16)
+
+    summaries()
+    fs = send(f_own, f_sib, sib)
+
     def z_hop(h, buf, rights, lefts):
         rights[h - 1].wait_recv()
         if h < 4:
@@ -136,6 +267,9 @@
     wlb.wait_recv()
     wfb = send(wbuf.at[s_xp, half_b], wbuf.at[s_xp, half_b], left["x"])
     ws.append(send(wbuf.at[s_xp, half_b], wbuf.at[s_xp, half_b], sib))
+    fs.wait_recv()
+    chip_state(f_own, f_sib, f_chip, c == 1)
+    far_send(f_chip, f_far, 0, 1)
     z_hop(2, zg, zgr, zgl)
     z_hop(3, zg, zgr, zgl)
     yxf = y_relay(xa, yx[0], yx[1])
@@ -264,6 +398,12 @@
     hb.wait_recv()
     add_rows(dxs.at[ym], yhb, HALF, D_EXT - HALF)
     fmb = send(dxs.at[ym, :, ext_b], yfp.at[:, ext_b], left["y"])
+    far_state(f_chip, f_far, f_sib, 0, 1, c == 1)
+    attention_main()
+    bs = send(b_own, b_sib, sib)
+    bs.wait_recv()
+    chip_state(b_own, b_sib, b_chip, c == 0)
+    far_send(b_chip, b_far, 6, -1)
     for copy in (fma, fpb, fpa, fmb):
         copy.wait_recv()
 
@@ -291,6 +431,8 @@
 
     zrc = [z_first(zr, right["z"], (z + 4) % 8)]
     zlc = [z_first(zl, left["z"], (z + 5) % 8)]
+    far_state(b_chip, b_far, b_sib, 6, -1, c == 0)
+    attention_last()
     for h in range(1, 4):
         nr, nl = [], []
         for n, p in enumerate(parts):
@@ -319,17 +461,23 @@
         )
     for copy in started:
         copy.wait_send()
-
-
-def expert_block(tok, grd, info, wall):
+    far_send(f_chip, f_far, 0, 1, finish=True)
+    far_send(b_chip, b_far, 6, -1, finish=True)
+
+
+def all_blocks(tok, grd, info, wall, q, k, v, probe, rate, gain, coef):
     bf16, f32 = jnp.bfloat16, jnp.float32
     vmem = pl.BlockSpec(memory_space=pltpu.VMEM)
-    n_copies = 66
+    n_copies = 68
+    grads = jax.ShapeDtypeStruct((2, BLOCK, 2 * HEAD), bf16)
+    states = pltpu.VMEM((2, 2, HEAD, HEAD), f32)
     return pl.pallas_call(
-        expert_kernel,
-        out_shape=jax.ShapeDtypeStruct((TOK, D_EXT), f32),
-        in_specs=[vmem, vmem, vmem, pl.BlockSpec(memory_space=pl.ANY)],
-        out_specs=vmem,
+        kernel,
+        out_shape=[jax.ShapeDtypeStruct((TOK, D_EXT), f32), grads, grads, grads],
+        in_specs=[vmem, vmem, vmem, pl.BlockSpec(memory_space=pl.ANY)]
+        + [vmem] * 4
+        + [pl.BlockSpec(memory_space=pltpu.SMEM), vmem, vmem],
+        out_specs=[vmem] * 4,
         scratch_shapes=[
             pltpu.VMEM((8, W_ROWS, N_ALL), bf16),
             pltpu.VMEM((8, TOK, D), bf16),
@@ -349,9 +497,18 @@
             pltpu.VMEM((4, TOK, D_EXT), bf16),
             pltpu.VMEM((3, TOK, D_EXT), bf16),
             pltpu.VMEM((CAP, 128), bf16),
+            states, states, pltpu.VMEM((2, HEAD, HEAD), f32),
+            states, states, pltpu.VMEM((2, HEAD, HEAD), f32),
+            pltpu.VMEM((3, 2, 2, HEAD, HEAD), f32),
+            pltpu.VMEM((3, 2, 2, HEAD, HEAD), f32),
+            states,
+            pltpu.VMEM((2, BLOCK, 2 * HEAD), f32),
+            pltpu.VMEM((2, BLOCK, 2 * HEAD), f32),
             pltpu.SemaphoreType.DMA((n_copies,)),
             pltpu.SemaphoreType.DMA((n_copies,)),
             pltpu.SemaphoreType.DMA((1,)),
+            pltpu.SemaphoreType.DMA((12,)),
+            pltpu.SemaphoreType.DMA((12,)),
         ],
         compiler_params=pltpu.CompilerParams(
             collective_id=0, has_side_effects=True, vmem_limit_bytes=64 * 1024 * 1024 - 65536
@@ -359,40 +516,8 @@
         cost_estimate=pl.CostEstimate(
             flops=12 * 10**9, bytes_accessed=40 * 10**6, transcendentals=200000
         ),
-        name="expert_block",
-    )(tok, grd, info, wall)
-
-
-def entering(x, axis, combine, identity, reverse):
-    length, here = (8, 2 * lax.axis_index("x") + lax.axis_index("c"))
-    everything = jax.tree.map(lambda part: lax.all_gather(part, axis), x)
-    start = jax.tree.map(
-        lambda part, zero: jnp.broadcast_to(jnp.asarray(zero, part.dtype), part.shape), x, identity
-    )
-
-    def lap(k, before):
-        at = length - 1 - k if reverse else k
-        reached = at > here if reverse else at < here
-        new = combine(before, jax.tree.map(lambda part: part[at], everything))
-        return jax.tree.map(lambda a, b: jnp.where(reached, a, b), new, before)
-
-    return lax.fori_loop(0, length, lap, start)
-
-
-def carry_combine(earlier, later):
-    return (earlier[0] * later[0], later[0] * earlier[1] + later[1])
-
-
-def earlier_state(summary, block_decay):
-    identity = (jnp.ones_like(block_decay), jnp.zeros_like(summary))
-    result = entering((block_decay, summary), AXES_SEQ, carry_combine, identity, False)
-    return result[1]
-
-
-def later_state(summary, block_decay):
-    identity = (jnp.ones_like(block_decay), jnp.zeros_like(summary))
-    result = entering((block_decay, summary), AXES_SEQ, carry_combine, identity, True)
-    return result[1]
+        name="all_blocks",
+    )(tok, grd, info, wall, q, k, v, probe, rate, gain, coef)
 
 
 def on_device(
@@ -416,66 +541,10 @@
     clip_high,
 ):
     rollouts, block_size, feature_width = queries.shape
-    head_count = decay_rate.shape[0]
-    head_size = feature_width // head_count
     importance = jnp.exp(trainer_logprob - rollout_logprob)
     clipped = jnp.minimum(jnp.maximum(importance, clip_low[0]), clip_high[0])
     coeff = -(clipped * advantage) / rollouts
     objective = coeff * trainer_logprob
-    shape_four = (rollouts, block_size, head_count, head_size)
-    query_full = queries.reshape(shape_four).astype(jnp.float32)
-    key_full = key_rows.reshape(shape_four).astype(jnp.float32)
-    value_full = value_rows.reshape(shape_four).astype(jnp.float32)
-    probe_full = attn_probe.reshape(shape_four).astype(jnp.float32)
-    gain_full = norm_gain.reshape(head_count, head_size)
-    offsets = jnp.arange(block_size, dtype=jnp.float32)
-    rate_row = decay_rate[None, :]
-    distance = offsets[:, None] - offsets[None, :]
-    within = jnp.where(
-        (distance >= 0)[None],
-        jnp.exp(-decay_rate[:, None, None] * jnp.maximum(distance, 0.0)[None]),
-        0.0,
-    )
-    lead_decay = jnp.exp(-rate_row * (offsets[:, None] + 1.0))[None, :, :, None]
-    key_tail = jnp.exp(-rate_row * (block_size - 1.0 - offsets[:, None]))[None, :, :, None]
-    query_tail = jnp.exp(-rate_row * offsets[:, None])[None, :, :, None]
-    grad_tail = jnp.exp(-rate_row * (block_size - offsets[:, None]))[None, :, :, None]
-    block_decay = jnp.exp(-decay_rate * block_size).reshape(1, head_count, 1, 1)
-    forward_summary = jnp.einsum(
-        "rjhk,rjhv->rhkv", key_full * key_tail, value_full, precision=highest
-    )
-    state_before = earlier_state(forward_summary, block_decay)
-    scores = jnp.einsum("rihc,rjhc->rhij", query_full, key_full, precision=highest) * within[None]
-    output = jnp.einsum("rhij,rjhv->rihv", scores, value_full, precision=highest)
-    output = output + lead_decay * jnp.einsum(
-        "rihk,rhkv->rihv", query_full, state_before, precision=highest
-    )
-    inverse = lax.rsqrt(jnp.mean(output * output, axis=-1, keepdims=True) + norm_epsilon)
-    scaled = gain_full[None, None] * (coeff[:, :, None, None] * probe_full)
-    grad_out = inverse * scaled - output * inverse**3 * jnp.mean(
-        scaled * output, axis=-1, keepdims=True
-    )
-    backward_summary = jnp.einsum(
-        "rihk,rihv->rhkv", query_full * query_tail, grad_out, precision=highest
-    )
-    state_after = later_state(backward_summary, block_decay)
-    product = jnp.einsum("rihv,rjhv->rhij", grad_out, value_full, precision=highest) * within[None]
-    grad_query = jnp.einsum("rhij,rjhk->rihk", product, key_full, precision=highest)
-    grad_query = grad_query + lead_decay * jnp.einsum(
-        "rihv,rhkv->rihk", grad_out, state_before, precision=highest
-    )
-    grad_key = jnp.einsum("rhij,rihk->rjhk", product, query_full, precision=highest)
-    grad_key = grad_key + grad_tail * jnp.einsum(
-        "rjhv,rhkv->rjhk", value_full, state_after, precision=highest
-    )
-    grad_value = jnp.einsum("rhij,rihv->rjhv", scores, grad_out, precision=highest)
-    grad_value = grad_value + grad_tail * jnp.einsum(
-        "rjhk,rhkv->rjhv", key_full, state_after, precision=highest
-    )
-    out_shape = (rollouts, block_size, feature_width)
-    grad_queries = grad_query.reshape(out_shape).astype(jnp.bfloat16)
-    grad_keys = grad_key.reshape(out_shape).astype(jnp.bfloat16)
-    grad_values = grad_value.reshape(out_shape).astype(jnp.bfloat16)
     positions, model_width = hidden_in.shape[1:]
     experts = router_weight.shape[1]
     z_index = lax.axis_index("z")
@@ -505,8 +574,11 @@
         ],
         axis=1,
     )
-    summed = expert_block(
-        hidden_in.reshape(TOK, model_width), grad_rows.reshape(TOK, model_width), info, wall
+    coef = jnp.broadcast_to(coeff[:, :, None], (rollouts, block_size, HEAD))
+    summed, grad_queries, grad_keys, grad_values = all_blocks(
+        hidden_in.reshape(TOK, model_width), grad_rows.reshape(TOK, model_width), info, wall,
+        queries, key_rows, value_rows, attn_probe, decay_rate, norm_gain.reshape(1, feature_width),
+        coef,
     )
     row_score = summed[:, model_width : model_width + experts].reshape(rollouts, positions, experts)
     score_pick = jnp.einsum("rpke,rpe->rpk", onehot, row_score, precision=highest)

time: 275 us -> 209 us (0.76)
  other arithmetic: 23.4 us -> 7.69 us
  between operations: 16.6 us -> 2.04 us
  blocking collectives: 11.3 us -> 0 us
  matrix products: 12.8 us -> 3.54 us
  local copies, waits for them, and re-layouts: 26.2 us -> 18 us
  Pallas kernels: 181 us -> 176 us
    select_n x17 -> x0, other arithmetic: 17 us -> none  [the longest x16 16.8 us: lap(): return jax.tree.map(lambda a, b: jnp.where(reached, a, b), new, before)]
    unnamed x1 -> x0, blocking collectives: 11.3 us -> none
    dot_general x13 -> x0, matrix products: 10.6 us -> none  [the longest x1 2.05 us: on_device(): jnp.einsum('rjhk,rjhv->rhkv', key_full * key_tail, value_full, precision=...]
    mul x16 -> x0, local copies, waits for them, and re-layouts: 5.18 us -> none  [carry_combine(): return (earlier[0] * later[0], later[0] * earlier[1] + later[1])]
    pallas_call x1, Pallas kernels: 181 us -> 176 us  [all_blocks(): pl.pallas_call(kernel, out_shape=[jax.ShapeDtypeStruct((TOK, D_EXT), f32)...]
    unnamed x79 -> x13, local copies, waits for them, and re-layouts: 9.39 us -> 10.2 us
  transfers between devices with their start and end apart: 2 -> 0, of which waited for: 1 -> 0; matrix products, arithmetic and copies ran while one was open for 9% -> 0% of each run, Pallas kernels for 66% -> 0%
where the time goes in v2:
time: 209 us; the launch traced here: 208 us
  Pallas kernels  176 us (84%)
  local copies, waits for them, and re-layouts  18 us (9%)
  other arithmetic  7.69 us (4%)
  matrix products  3.54 us (2%)
    pallas_call x1, Pallas kernels, all_blocks(): pl.pallas_call(kernel, out_shape=[jax.ShapeDtypeStruct((TOK, D_EXT), f32)...  176 us
    unnamed x13, local copies, waits for them, and re-layouts  10.2 us
    concatenate x1, local copies, waits for them, and re-layouts, on_device(): jnp.concatenate([gate[:, :H_MAIN], up[:, :H_MAIN], gate[:, H_MAIN:], up[:...  4.4 us

profile of v2, /device:TPU:6, one launch (start us, length us, event | category | flops | bytes accessed | tf_op | source)
XLA Modules:
  0.0 207.6 jit_solution(10197059840459409103)
XLA Ops:
  1.9 1.3 fusion.6
  3.2 0.1 constant_dynamic-slice_fusion
  3.3 1.7 fusion.1.grd
  5.0 1.5 fusion.3
  6.5 0.7 select_reduce_fusion.3
  7.2 0.0 copy-start
  7.2 0.5 copy-done
  7.7 0.0 copy-start.1
  7.7 0.7 convert_reduce_fusion
  8.4 0.0 copy-done.1
  8.4 0.4 reduce_window_sum.11
  8.8 0.1 add_select_fusion
  8.9 0.1 reshape.40
  9.0 0.2 dynamic_update_slice.3.info
  9.2 0.0 copy-start.2
  9.2 1.5 copy.29
  10.7 0.0 copy-done.2
  10.7 0.1 slice.24
  10.8 1.5 copy.30
  12.4 0.1 slice.25
  12.4 0.7 slice.26
  13.1 0.7 slice.27
  13.8 1.5 copy.31
  15.4 4.4 %concatenate.7.wall = bf16[768,1792]{1,0:T(8,128)(2,1)} concatenate(bf16[768,512]{1,0:T(8,128)(2,1)S(1)} %slice.24, bf16[768,512]{1,0:T(8,128)(2,1)S(1)} %slice.25, bf16[768,64]{1,0:T(8,128)(2,1)} %slice.26, bf16[768,64]{1,0:T(8,128)(2,1)} %slice.27, bf16[768,576]{1,0:T(8,128)(2,1)S(1)} %bitcast.36, bf16[768,64]{1,0:T(8,128)(2,1)S(1)} %broadcast_in_dim.9), dimensions={1} | concatenate | bytes 5505024 | tf_op jit(solution)/shard_map/concatenate | solution.py:570
  19.8 0.8 broadcast_in_dim.10.coef
  20.6 176.4 %all_blocks.1 = (f32[16,6272]{1,0:T(8,128)}, bf16[2,256,256]{2,1,0:T(8,128)(2,1)}, bf16[2,256,256]{2,1,0:T(8,128)(2,1)}, bf16[2,256,256]{2,1,0:T(8,128)(2,1)}) custom-call(bf16[16,6144]{1,0:T(8,128)(2,1)} %bitcast.38, bf16[16,6144]{1,0:T(8,128)(2,1)} %fusion.1.grd, f32[8,128]{1,0:T(8,128)} %copy-done.2, bf16[768,1792]{1,0:T(8,128)(2,1)} %concatenate.7.wall, ...), custom_call_target="tpu_custom_call" | custom-call | flops 12000000000 | bytes 40000000 | tf_op jit(solution)/shard_map/all_blocks/pallas_call | solution.py:474
  197.0 0.7 slice_bitcast_fusion
  197.7 0.1 copy.59
  197.8 0.7 select_reduce_fusion.1
  198.5 0.7 multiply_reduce_fusion
  199.2 0.7 subtract_multiply_fusion
  199.8 0.7 select_reduce_fusion
  200.5 2.1 %fusion = bf16[2,8,6144]{2,1,0:T(8,128)(2,1)} fusion(f32[2,8,4]{1,2,0:T(4,128)S(1)} %select_reduce_fusion, f32[16,6272]{1,0:T(8,128)} %get-tuple-element.12, bf16[6144,4]{0,1:T(4,128)(2,1)} %param.26), kind=kOutput, calls=%fused_computation.1 | convolution fusion | flops 4915200 | bytes 639232 | tf_op jit(solution)/shard_map/rpe,de->rpd/dot_general | solution.py:589
  202.6 1.7 copy.69
  204.3 1.7 copy.70
  206.0 1.7 copy.71
  (7 shorter events, 0.1 us)
Async XLA Ops:
  7.2 0.5 copy-start
  7.7 0.7 copy-start.1
  9.2 1.6 copy-start.2

commit v3 on v2

--- a/solution.py
+++ b/solution.py
@@ -5,7 +5,6 @@
 from jax.experimental.pallas import tpu as pltpu
 from jax.sharding import Mesh, PartitionSpec as P
 
-highest = lax.Precision.HIGHEST
 norm_epsilon = 1e-06
 MESH = pl.DeviceIdType.MESH
 AXES_SEQ = ("x", "c")
@@ -25,8 +24,10 @@
 
 
 def kernel(
-    tok, grd, info, wall, qr, kr, vr, pr, rate, gain, coef,
-    out, gq, gk, gv,
+    tok, moe, router, route, gate_w, up_w, down_w, qr, kr, vr, pr, rate, gain,
+    roll_lp, train_lp, adv, low, high,
+    obj, gh, gq, gk, gv,
+    coef, coef_tok, grd, info, gates, wraw, out,
     wbuf, zx, zg, zi, xa, ga, pre, ugr, ggu, dxs, yha, yhb, yfp, yfm, cz, zr, zl, psel,
     f_own, f_sib, f_chip, b_own, b_sib, b_chip, f_far, b_far, state, dk_part, dv_part,
     ssem, rsem, lsem, xss, xrs,
@@ -51,6 +52,12 @@
         started.append(copy)
         return copy
 
+    raw = [
+        pltpu.make_async_copy(w.at[0], wraw.at[n], lsem.at[n])
+        for n, w in enumerate((gate_w, up_w, down_w))
+    ]
+    for copy in raw:
+        copy.start()
     barrier = pltpu.get_barrier_semaphore()
     peers = [right[a] for a in "xyz"] + [left[a] for a in "xyz"] + [sib]
     peers += [{"x": xp, "c": 1 - c}, {"x": xm, "c": 1 - c}, {"x": (x + 2) % 4}]
@@ -59,23 +66,35 @@
         pl.semaphore_signal(barrier, inc=1, device_id=peer, device_id_type=MESH)
     pl.semaphore_wait(barrier, len(peers))
 
-    half_a, half_b = pl.ds(0, W_ROWS // 2), pl.ds(W_ROWS // 2, W_ROWS // 2)
-    wra = send(wall.at[half_a], wbuf.at[me, half_a], right["x"])
-    wlb = send(wall.at[half_b], wbuf.at[me, half_b], left["x"])
+    zx[z] = tok[...]
     zxr = [send(tok, zx.at[z], right["z"])]
     zxl = [send(tok, zx.at[z], left["z"])]
-    zir = [send(info, zi.at[z], right["z"])]
-    zil = [send(info, zi.at[z], left["z"])]
-    wrb = send(wall.at[half_b], wbuf.at[me, half_b], right["x"])
-    wla = send(wall.at[half_a], wbuf.at[me, half_a], left["x"])
-    ws = [send(wall, wbuf.at[me], sib)]
-    own = pltpu.make_async_copy(wall, wbuf.at[me], lsem.at[0])
-    own.start()
-    zx[z] = tok[...]
-    zg[z] = grd[...]
-    zi[z] = info[...]
-    pre[...] = jnp.zeros_like(pre)
-    ugr[...] = jnp.zeros_like(ugr)
+
+    for copy in raw:
+        copy.wait()
+
+    def pack(first):
+        @pl.loop(0, W_ROWS // 128)
+        def _(i):
+            r = pl.ds(pl.multiple_of(first + i * 64, 64), 64)
+            wbuf[me, r, 0:512] = wraw[0, r, 0:512]
+            wbuf[me, r, 512:1024] = wraw[1, r, 0:512]
+            wbuf[me, r, 1024:1152] = jnp.concatenate(
+                [wraw[0, r, 512:576], wraw[1, r, 512:576]], axis=1
+            )
+            wbuf[me, r, 1152:1664] = wraw[2, r, 0:512]
+            wbuf[me, r, 1664:1792] = jnp.concatenate(
+                [wraw[2, r, 512:576], jnp.zeros((64, 64), jnp.bfloat16)], axis=1
+            )
+
+    half_a, half_b = pl.ds(0, W_ROWS // 2), pl.ds(W_ROWS // 2, W_ROWS // 2)
+    pack(0)
+    wra = send(wbuf.at[me, half_a], wbuf.at[me, half_a], right["x"])
+    pack(W_ROWS // 2)
+    wlb = send(wbuf.at[me, half_b], wbuf.at[me, half_b], left["x"])
+    wrb = send(wbuf.at[me, half_b], wbuf.at[me, half_b], right["x"])
+    wla = send(wbuf.at[me, half_a], wbuf.at[me, half_a], left["x"])
+    ws = [send(wbuf.at[me], wbuf.at[me], sib)]
 
     f32, bf16 = jnp.float32, jnp.bfloat16
     nn, nt, tn = (((1,), (0,)), ((), ())), (((1,), (1,)), ((), ())), (((0,), (0,)), ((), ()))
@@ -200,6 +219,52 @@
             gk[r, :, lanes(h)] = dk.astype(bf16)
             gv[r, :, lanes(h)] = dv.astype(bf16)
 
+    lane = lax.broadcasted_iota(jnp.int32, (TOK, 128), 1)
+    token = lax.broadcasted_iota(jnp.int32, (TOK, 128), 0)
+    member = jnp.logical_or(lane == route[:, 0:1], lane == route[:, 1:2])
+    t_row = lax.broadcasted_iota(jnp.int32, (TOK, TOK), 0)
+    t_col = lax.broadcasted_iota(jnp.int32, (TOK, TOK), 1)
+    ahead = jnp.logical_and(t_col < t_row, (t_col >= 8) == (t_row >= 8))
+    rank = mm(ahead.astype(f32).astype(bf16), member.astype(f32).astype(bf16), nn)
+    slot = rank + jnp.where(token >= 8, 6.0, 1.0) + (10 * z).astype(f32)
+    slot = jnp.where(member, slot, 0.0)
+    gates[...] = jnp.zeros_like(gates)
+    gates[:, 0:4] = mm(tok[...], router[...], nn)
+    weight = jnp.where(member, jnp.exp(gates[...]), 0.0)
+    gate = weight / jnp.sum(weight, axis=1, keepdims=True)
+    gates[...] = gate
+    a_high, a_low = parts_of(slot + pltpu.roll(gate, 4, 1))
+    place = (lane == token + TOK * z).astype(f32).astype(bf16)
+    info[...] = (mm(a_high, place, tn) + mm(a_low, place, tn))[0:8]
+    zi[z] = info[...]
+    zir = [send(info, zi.at[z], right["z"])]
+    zil = [send(info, zi.at[z], left["z"])]
+
+    ratio = jnp.exp(train_lp[...] - roll_lp[...])
+    ratio = jnp.minimum(jnp.maximum(ratio, low[0]), high[0])
+    coeff = -(ratio * adv[...]) / 2.0
+    obj[...] = coeff * train_lp[...]
+    eye = lax.broadcasted_iota(jnp.int32, (128, 128), 0) == lax.broadcasted_iota(
+        jnp.int32, (128, 128), 1
+    )
+    for r in range(2):
+        for part in range(2):
+            row = jnp.broadcast_to(coeff[r : r + 1, 128 * part : 128 * part + 128], (128, 128))
+            col = jnp.sum(jnp.where(eye, row, 0.0), axis=1, keepdims=True)
+            coef[r, 128 * part : 128 * part + 128, :] = jnp.broadcast_to(col, (128, 128))
+    here = pl.ds(pl.multiple_of(8 * (4 * z + y), 8), 8)
+    for r in range(2):
+        coef_tok[8 * r : 8 * r + 8, :] = coef[r, here, :]
+
+    @pl.loop(0, D // 512)
+    def _(i):
+        cols = pl.ds(pl.multiple_of(i * 512, 512), 512)
+        grad = moe[:, cols].astype(f32) * coef_tok[:, 0:1]
+        grd[:, cols] = grad.astype(bf16)
+        zg[z, :, cols] = grad.astype(bf16)
+
+    pre[...] = jnp.zeros_like(pre)
+    ugr[...] = jnp.zeros_like(ugr)
     summaries()
     fs = send(f_own, f_sib, sib)
 
@@ -302,7 +367,6 @@
                 preferred_element_type=jnp.float32,
             )
 
-    own.wait()
     for copy in ws:
         copy.wait_recv()
     ws_done = len(ws)
@@ -332,8 +396,6 @@
     s_x2o = 2 * ((x + 2) % 4) + 1 - c
     add_in(s_x2o)
     add_out(s_x2o)
-
-    lane = lax.broadcasted_iota(jnp.int32, (TOK, 128), 1)
 
     def grads(gate, up, unit):
         sig = jax.nn.sigmoid(gate)
@@ -459,26 +521,76 @@
             + zr[3, :, p].astype(jnp.float32)
             + zl[2, :, p].astype(jnp.float32)
         )
+
+    score = out[:, D:D_EXT]
+    gate = gates[...]
+    logit = gate * (score - jnp.sum(gate * score, axis=1, keepdims=True))
+    l_high, l_low = parts_of(logit[:, 0:4])
+
+    @pl.loop(0, D // 512)
+    def _(i):
+        cols = pl.ds(pl.multiple_of(i * 512, 512), 512)
+        to_hidden = mm(l_high, router[cols, :], nt) + mm(l_low, router[cols, :], nt)
+        gh[:, cols] = (out[:, cols] + to_hidden).astype(bf16)
+
     for copy in started:
         copy.wait_send()
     far_send(f_chip, f_far, 0, 1, finish=True)
     far_send(b_chip, b_far, 6, -1, finish=True)
 
 
-def all_blocks(tok, grd, info, wall, q, k, v, probe, rate, gain, coef):
+def copy_out(*refs):
+    n = len(refs) // 3
+    sem = refs[-1]
+    ins, outs, bufs = refs[:n], refs[n : 2 * n], refs[2 * n : 3 * n]
+    arrive = [pltpu.make_async_copy(ins[i], bufs[i], sem.at[i]) for i in range(n)]
+    leave = [pltpu.make_async_copy(bufs[i], outs[i], sem.at[n + i]) for i in range(n)]
+    for copy in arrive:
+        copy.start()
+    for i in range(n):
+        arrive[i].wait()
+        leave[i].start()
+    for copy in leave:
+        copy.wait()
+
+
+def results(*arrays):
+    n = len(arrays)
+    where = pl.BlockSpec(memory_space=pl.ANY)
+    return pl.pallas_call(
+        copy_out,
+        out_shape=[jax.ShapeDtypeStruct(a.shape, a.dtype) for a in arrays],
+        in_specs=[where] * n,
+        out_specs=[where] * n,
+        scratch_shapes=[pltpu.VMEM(a.shape, a.dtype) for a in arrays]
+        + [pltpu.SemaphoreType.DMA((2 * n,))],
+        name="results",
+    )(*arrays)
+
+
+def all_blocks(*operands):
     bf16, f32 = jnp.bfloat16, jnp.float32
-    vmem = pl.BlockSpec(memory_space=pltpu.VMEM)
+    vmem, smem = (pl.BlockSpec(memory_space=m) for m in (pltpu.VMEM, pltpu.SMEM))
+    hbm = pl.BlockSpec(memory_space=pl.ANY)
     n_copies = 68
     grads = jax.ShapeDtypeStruct((2, BLOCK, 2 * HEAD), bf16)
     states = pltpu.VMEM((2, 2, HEAD, HEAD), f32)
     return pl.pallas_call(
         kernel,
-        out_shape=[jax.ShapeDtypeStruct((TOK, D_EXT), f32), grads, grads, grads],
-        in_specs=[vmem, vmem, vmem, pl.BlockSpec(memory_space=pl.ANY)]
-        + [vmem] * 4
-        + [pl.BlockSpec(memory_space=pltpu.SMEM), vmem, vmem],
-        out_specs=[vmem] * 4,
+        out_shape=[
+            jax.ShapeDtypeStruct((2, BLOCK), f32), jax.ShapeDtypeStruct((TOK, D), bf16),
+            grads, grads, grads,
+        ],
+        in_specs=[vmem] * 4 + [hbm] * 3 + [vmem] * 4 + [smem] + [vmem] * 4 + [smem] * 2,
+        out_specs=[vmem] * 5,
         scratch_shapes=[
+            pltpu.VMEM((2, BLOCK, 128), f32),
+            pltpu.VMEM((TOK, 128), f32),
+            pltpu.VMEM((TOK, D), bf16),
+            pltpu.VMEM((8, 128), f32),
+            pltpu.VMEM((TOK, 128), f32),
+            pltpu.VMEM((3, W_ROWS, H_MAIN + H_TAIL), bf16),
+            pltpu.VMEM((TOK, D_EXT), f32),
             pltpu.VMEM((8, W_ROWS, N_ALL), bf16),
             pltpu.VMEM((8, TOK, D), bf16),
             pltpu.VMEM((8, TOK, D), bf16),
@@ -506,7 +618,7 @@
             pltpu.VMEM((2, BLOCK, 2 * HEAD), f32),
             pltpu.SemaphoreType.DMA((n_copies,)),
             pltpu.SemaphoreType.DMA((n_copies,)),
-            pltpu.SemaphoreType.DMA((1,)),
+            pltpu.SemaphoreType.DMA((3,)),
             pltpu.SemaphoreType.DMA((12,)),
             pltpu.SemaphoreType.DMA((12,)),
         ],
@@ -517,7 +629,7 @@
             flops=12 * 10**9, bytes_accessed=40 * 10**6, transcendentals=200000
         ),
         name="all_blocks",
-    )(tok, grd, info, wall, q, k, v, probe, rate, gain, coef)
+    )(*operands)
 
 
 def on_device(
@@ -540,56 +652,15 @@
     clip_low,
     clip_high,
 ):
-    rollouts, block_size, feature_width = queries.shape
-    importance = jnp.exp(trainer_logprob - rollout_logprob)
-    clipped = jnp.minimum(jnp.maximum(importance, clip_low[0]), clip_high[0])
-    coeff = -(clipped * advantage) / rollouts
-    objective = coeff * trainer_logprob
-    positions, model_width = hidden_in.shape[1:]
-    experts = router_weight.shape[1]
-    z_index = lax.axis_index("z")
-    local_coeff = lax.dynamic_slice_in_dim(
-        coeff, (4 * z_index + lax.axis_index("y")) * positions, positions, 1
+    rollouts, positions, width = hidden_in.shape
+    objective, *rest = all_blocks(
+        hidden_in.reshape(TOK, width), moe_probe.reshape(TOK, width), router_weight,
+        routes.reshape(TOK, 2), gate_weight, up_weight, down_weight,
+        queries, key_rows, value_rows, attn_probe, decay_rate, norm_gain.reshape(1, -1),
+        rollout_logprob, trainer_logprob, advantage, clip_low, clip_high,
     )
-    grad_rows = (local_coeff[:, :, None] * moe_probe.astype(jnp.float32)).astype(jnp.bfloat16)
-    onehot = (routes[..., None] == jnp.arange(experts, dtype=jnp.int32)).astype(jnp.float32)
-    member = onehot.sum(axis=2)
-    rank = jnp.cumsum(member, axis=1) - member
-    slot = rank + 5.0 * jnp.arange(rollouts, dtype=jnp.float32)[:, None, None]
-    slot = jnp.where(member > 0, slot + 1.0 + (10 * z_index).astype(jnp.float32), 0.0)
-    logits = jnp.einsum("rpd,de->rpe", hidden_in, router_weight, preferred_element_type=jnp.float32)
-    chosen = jnp.einsum("rpke,rpe->rpk", onehot, logits, precision=highest)
-    exponent = jnp.exp(chosen)
-    gates = exponent / jnp.sum(exponent, axis=-1, keepdims=True)
-    gate_expert = jnp.einsum("rpk,rpke->rpe", gates, onehot, precision=highest)
-    both = jnp.concatenate([slot, gate_expert], axis=2).reshape(TOK, 2 * experts).T
-    info = lax.dynamic_update_slice(
-        jnp.zeros((2 * experts, 128), jnp.float32), both, (0, TOK * z_index)
-    )
-    gate, up, down = gate_weight[0], up_weight[0], down_weight[0]
-    wall = jnp.concatenate(
-        [
-            gate[:, :H_MAIN], up[:, :H_MAIN], gate[:, H_MAIN:], up[:, H_MAIN:],
-            down, jnp.zeros((W_ROWS, H_TAIL), jnp.bfloat16),
-        ],
-        axis=1,
-    )
-    coef = jnp.broadcast_to(coeff[:, :, None], (rollouts, block_size, HEAD))
-    summed, grad_queries, grad_keys, grad_values = all_blocks(
-        hidden_in.reshape(TOK, model_width), grad_rows.reshape(TOK, model_width), info, wall,
-        queries, key_rows, value_rows, attn_probe, decay_rate, norm_gain.reshape(1, feature_width),
-        coef,
-    )
-    row_score = summed[:, model_width : model_width + experts].reshape(rollouts, positions, experts)
-    score_pick = jnp.einsum("rpke,rpe->rpk", onehot, row_score, precision=highest)
-    score_mean = jnp.sum(gates * score_pick, axis=-1, keepdims=True)
-    logit_grad = gates * (score_pick - score_mean)
-    logit_expert = jnp.einsum("rpk,rpke->rpe", logit_grad, onehot, precision=highest)
-    grad_hidden = summed[:, :model_width].reshape(rollouts, positions, model_width)
-    grad_hidden = grad_hidden + jnp.einsum(
-        "rpe,de->rpd", logit_expert, router_weight.astype(jnp.float32), precision=highest
-    )
-    return (objective, grad_queries, grad_keys, grad_values, grad_hidden.astype(jnp.bfloat16))
+    objective, grad_hidden, *grads = results(objective, *rest)
+    return (objective, *grads, grad_hidden.reshape(rollouts, positions, width))
 
 
 def solution(mesh):

time: 209 us -> 192 us (0.919)
  local copies, waits for them, and re-layouts: 18 us -> 7.9 us
  other arithmetic: 7.69 us -> 0 us
  Pallas kernels: 176 us -> 182 us
  matrix products: 3.54 us -> 0 us
    pallas_call x1 -> x2, Pallas kernels: 176 us -> 182 us  [the longest x1 180 us: all_blocks(): pl.pallas_call(kernel, out_shape=[jax.ShapeDtypeStruct((2, BLOCK), f32),...]
    concatenate x2 -> x0, local copies, waits for them, and re-layouts: 4.41 us -> none  [the longest x1 4.4 us: on_device(): jnp.concatenate([gate[:, :H_MAIN], up[:, :H_MAIN], gate[:, H_MAIN:], up[:...]
    unnamed x13 -> x10, local copies, waits for them, and re-layouts: 10.2 us -> 6.54 us
    dot_general x3 -> x0, other arithmetic: 2.12 us -> none  [the longest x1 0.72 us: on_device(): chosen = jnp.einsum('rpke,rpe->rpk', onehot, logits, precision=highest)]
where the time goes in v3:
time: 192 us
  Pallas kernels  182 us (95%)
  local copies, waits for them, and re-layouts  7.9 us (4%)
  between operations  2.02 us (1%)
    pallas_call x1, Pallas kernels, all_blocks(): pl.pallas_call(kernel, out_shape=[jax.ShapeDtypeStruct((2, BLOCK), f32),...  180 us
    unnamed x10, local copies, waits for them, and re-layouts  6.54 us

profile of v3, /device:TPU:6, one launch (start us, length us, event | category | flops | bytes accessed | tf_op | source)
XLA Modules:
  0.0 191.7 jit_solution(4836953210069251892)
XLA Ops:
  0.6 0.0 copy-start
  2.0 1.4 copy.29
  3.4 0.0 copy-start.1
  3.4 2.3 %copy.26.gate_w = bf16[1,768,576]{2,1,0:T(8,128)(2,1)} copy(bf16[1,768,576]{1,2,0:T(8,128)(2,1)} %param.28) | data formatting | bytes 1769472 | tf_op args[10]
  5.7 0.0 copy-done
  5.7 0.0 copy-start.2
  5.7 1.3 copy.27.up_w
  7.0 0.0 copy-done.1
  7.0 1.3 copy.28.down_w
  8.3 0.0 copy-done.2
  8.3 1.6 copy.24.router
  9.9 179.7 %all_blocks.1 = (f32[2,256]{1,0:T(2,128)}, bf16[16,6144]{1,0:T(8,128)(2,1)}, bf16[2,256,256]{2,1,0:T(8,128)(2,1)}, bf16[2,256,256]{2,1,0:T(8,128)(2,1)}, bf16[2,256,256]{2,1,0:T(8,128)(2,1)}) custom-call(bf16[16,6144]{1,0:T(8,128)(2,1)} %bitcast.6, bf16[16,6144]{1,0:T(8,128)(2,1)} %bitcast.7, bf16[6144,4]{1,0:T(8,128)(2,1)} %copy.24.router, ...), custom_call_target="tpu_custom_call" | custom-call | flops 12000000000 | bytes 40000000 | tf_op jit(solution)/shard_map/all_blocks/pallas_call | solution.py:578
  189.6 2.0 %results.1 = (f32[2,256]{1,0:T(2,128)}, bf16[16,6144]{1,0:T(8,128)(2,1)}, bf16[2,256,256]{2,1,0:T(8,128)(2,1)}, bf16[2,256,256]{2,1,0:T(8,128)(2,1)}, bf16[2,256,256]{2,1,0:T(8,128)(2,1)}) custom-call(f32[2,256]{1,0:T(2,128)} %get-tuple-element.15.refs_0_, bf16[16,6144]{1,0:T(8,128)(2,1)} %get-tuple-element.16.refs_1_, ...), custom_call_target="tpu_custom_call" | custom-call | tf_op jit(solution)/shard_map/results/pallas_call | solution.py:560
Async XLA Ops:
  0.6 5.0 %copy-start = (bf16[1,768,576]{1,2,0:T(8,128)(2,1)S(1)}, bf16[1,768,576]{1,2,0:T(8,128)(2,1)}, u32[]{:S(2)}) copy-start(bf16[1,768,576]{1,2,0:T(8,128)(2,1)} %param.29) | copy-start | bytes 2654212
  3.4 3.6 %copy-start.1 = (bf16[1,768,576]{1,2,0:T(8,128)(2,1)S(1)}, bf16[1,768,576]{1,2,0:T(8,128)(2,1)}, u32[]{:S(2)}) copy-start(bf16[1,768,576]{1,2,0:T(8,128)(2,1)} %param.30) | copy-start | bytes 2654212
  5.7 2.6 %copy-start.2 = (bf16[6144,4]{0,1:T(4,128)(2,1)S(1)}, bf16[6144,4]{0,1:T(4,128)(2,1)}, u32[]{:S(2)}) copy-start(bf16[6144,4]{0,1:T(4,128)(2,1)} %param.26) | copy-start | bytes 147460

commit v4 on v3

--- a/solution.py
+++ b/solution.py
@@ -11,11 +11,12 @@
 AXES_EXPERT = ("z", "y")
 
 D = 6144
-W_ROWS = 768
+W_COLS = 768
+UNITS = 576
 H_MAIN = 512
-H_TAIL = 64
 N_IN = 1152
-N_ALL = 1792
+N_ALL = 1728
+U_PAD = 640
 TOK = 16
 CAP = 80
 HALF = 3072
@@ -27,8 +28,8 @@
     tok, moe, router, route, gate_w, up_w, down_w, qr, kr, vr, pr, rate, gain,
     roll_lp, train_lp, adv, low, high,
     obj, gh, gq, gk, gv,
-    coef, coef_tok, grd, info, gates, wraw, out,
-    wbuf, zx, zg, zi, xa, ga, pre, ugr, ggu, dxs, yha, yhb, yfp, yfm, cz, zr, zl, psel,
+    coef, coef_tok, route_tok, grd, info, gates, out,
+    wbuf, zx, zg, zi, xa, ga, pre, ugr, ggu, dxs, yh, yfp, yfm, cz, zr, zl, psel,
     f_own, f_sib, f_chip, b_own, b_sib, b_chip, f_far, b_far, state, dk_part, dv_part,
     ssem, rsem, lsem, xss, xrs,
 ):
@@ -53,8 +54,16 @@
         return copy
 
     raw = [
-        pltpu.make_async_copy(w.at[0], wraw.at[n], lsem.at[n])
-        for n, w in enumerate((gate_w, up_w, down_w))
+        pltpu.make_async_copy(
+            w.at[0, pl.ds(src, n)], wbuf.at[me, pl.ds(dst, n)], lsem.at[i]
+        )
+        for i, (w, src, dst, n) in enumerate((
+            (gate_w, 0, 0, H_MAIN),
+            (up_w, 0, H_MAIN, H_MAIN),
+            (gate_w, H_MAIN, 2 * H_MAIN, UNITS - H_MAIN),
+            (up_w, H_MAIN, H_MAIN + UNITS, UNITS - H_MAIN),
+            (down_w, 0, N_IN, UNITS),
+        ))
     ]
     for copy in raw:
         copy.start()
@@ -66,31 +75,22 @@
         pl.semaphore_signal(barrier, inc=1, device_id=peer, device_id_type=MESH)
     pl.semaphore_wait(barrier, len(peers))
 
+    col_a, col_b = pl.ds(0, HALF), pl.ds(HALF, HALF)
     zx[z] = tok[...]
-    zxr = [send(tok, zx.at[z], right["z"])]
-    zxl = [send(tok, zx.at[z], left["z"])]
-
+
+    def z_own(src, dst, dev):
+        return [[send(src.at[:, p], dst.at[z, :, p], dev) for p in (col_a, col_b)]]
+
+    zxr = z_own(tok, zx, right["z"])
+    zxl = z_own(tok, zx, left["z"])
+
+    half = N_ALL // 2
+    half_a, half_b = pl.ds(0, half), pl.ds(half, half)
+    quarters_a = pl.ds(0, half // 2), pl.ds(half // 2, half // 2)
+    quarters_b = pl.ds(half, half // 2), pl.ds(half + half // 2, half // 2)
     for copy in raw:
         copy.wait()
-
-    def pack(first):
-        @pl.loop(0, W_ROWS // 128)
-        def _(i):
-            r = pl.ds(pl.multiple_of(first + i * 64, 64), 64)
-            wbuf[me, r, 0:512] = wraw[0, r, 0:512]
-            wbuf[me, r, 512:1024] = wraw[1, r, 0:512]
-            wbuf[me, r, 1024:1152] = jnp.concatenate(
-                [wraw[0, r, 512:576], wraw[1, r, 512:576]], axis=1
-            )
-            wbuf[me, r, 1152:1664] = wraw[2, r, 0:512]
-            wbuf[me, r, 1664:1792] = jnp.concatenate(
-                [wraw[2, r, 512:576], jnp.zeros((64, 64), jnp.bfloat16)], axis=1
-            )
-
-    half_a, half_b = pl.ds(0, W_ROWS // 2), pl.ds(W_ROWS // 2, W_ROWS // 2)
-    pack(0)
     wra = send(wbuf.at[me, half_a], wbuf.at[me, half_a], right["x"])
-    pack(W_ROWS // 2)
     wlb = send(wbuf.at[me, half_b], wbuf.at[me, half_b], left["x"])
     wrb = send(wbuf.at[me, half_b], wbuf.at[me, half_b], right["x"])
     wla = send(wbuf.at[me, half_a], wbuf.at[me, half_a], left["x"])
@@ -177,8 +177,8 @@
                 near = sib_ref[r, h] + block_decay(h, 1) * far
                 state[r, h] = jnp.where(with_sib, near, far)
 
-    def attention_main():
-        @pl.loop(0, 4)
+    def attention_main(first, end):
+        @pl.loop(first, end)
         def _(i):
             r, h = i // 2, i % 2
             query, key, value = qr[r, :, lanes(h)], kr[r, :, lanes(h)], vr[r, :, lanes(h)]
@@ -221,7 +221,16 @@
 
     lane = lax.broadcasted_iota(jnp.int32, (TOK, 128), 1)
     token = lax.broadcasted_iota(jnp.int32, (TOK, 128), 0)
-    member = jnp.logical_or(lane == route[:, 0:1], lane == route[:, 1:2])
+    eye = lax.broadcasted_iota(jnp.int32, (128, 128), 0) == lax.broadcasted_iota(
+        jnp.int32, (128, 128), 1
+    )
+    for r in range(2):
+        for j in range(2):
+            row = jnp.broadcast_to(route[r, j : j + 1, :].astype(f32), (8, 8))
+            col = jnp.sum(jnp.where(eye[0:8, 0:8], row, 0.0), axis=1, keepdims=True)
+            route_tok[j, 8 * r : 8 * r + 8, :] = jnp.broadcast_to(col, (8, 128))
+    lane_f = lane.astype(f32)
+    member = jnp.logical_or(lane_f == route_tok[0], lane_f == route_tok[1])
     t_row = lax.broadcasted_iota(jnp.int32, (TOK, TOK), 0)
     t_col = lax.broadcasted_iota(jnp.int32, (TOK, TOK), 1)
     ahead = jnp.logical_and(t_col < t_row, (t_col >= 8) == (t_row >= 8))
@@ -229,7 +238,7 @@
     slot = rank + jnp.where(token >= 8, 6.0, 1.0) + (10 * z).astype(f32)
     slot = jnp.where(member, slot, 0.0)
     gates[...] = jnp.zeros_like(gates)
-    gates[:, 0:4] = mm(tok[...], router[...], nn)
+    gates[:, 0:4] = mm(tok[...], router[...], nt)
     weight = jnp.where(member, jnp.exp(gates[...]), 0.0)
     gate = weight / jnp.sum(weight, axis=1, keepdims=True)
     gates[...] = gate
@@ -237,16 +246,13 @@
     place = (lane == token + TOK * z).astype(f32).astype(bf16)
     info[...] = (mm(a_high, place, tn) + mm(a_low, place, tn))[0:8]
     zi[z] = info[...]
-    zir = [send(info, zi.at[z], right["z"])]
-    zil = [send(info, zi.at[z], left["z"])]
+    zir = [[send(info, zi.at[z], right["z"])]]
+    zil = [[send(info, zi.at[z], left["z"])]]
 
     ratio = jnp.exp(train_lp[...] - roll_lp[...])
     ratio = jnp.minimum(jnp.maximum(ratio, low[0]), high[0])
     coeff = -(ratio * adv[...]) / 2.0
     obj[...] = coeff * train_lp[...]
-    eye = lax.broadcasted_iota(jnp.int32, (128, 128), 0) == lax.broadcasted_iota(
-        jnp.int32, (128, 128), 1
-    )
     for r in range(2):
         for part in range(2):
             row = jnp.broadcast_to(coeff[r : r + 1, 128 * part : 128 * part + 128], (128, 128))
@@ -268,22 +274,27 @@
     summaries()
     fs = send(f_own, f_sib, sib)
 
-    def z_hop(h, buf, rights, lefts):
-        rights[h - 1].wait_recv()
-        if h < 4:
-            at = (z + 8 - h) % 8
-            rights.append(send(buf.at[at], buf.at[at], right["z"]))
-        if h <= 3:
-            lefts[h - 1].wait_recv()
-            if h < 3:
-                at = (z + h) % 8
-                lefts.append(send(buf.at[at], buf.at[at], left["z"]))
-
+    def z_hop(h, buf, rights, lefts, pieces):
+        nr, nl = [], []
+        for n, p in enumerate(pieces):
+            rights[h - 1][n].wait_recv()
+            if h < 4:
+                at = (z + 8 - h) % 8
+                nr.append(send(buf.at[at, :, p], buf.at[at, :, p], right["z"]))
+            if h <= 3:
+                lefts[h - 1][n].wait_recv()
+                if h < 3:
+                    at = (z + h) % 8
+                    nl.append(send(buf.at[at, :, p], buf.at[at, :, p], left["z"]))
+        rights.append(nr)
+        lefts.append(nl)
+
+    halves, whole = (col_a, col_b), (pl.ds(0, 128),)
     for h in range(1, 5):
-        z_hop(h, zx, zxr, zxl)
-        z_hop(h, zi, zir, zil)
-    zgr = [send(grd, zg.at[z], right["z"])]
-    zgl = [send(grd, zg.at[z], left["z"])]
+        z_hop(h, zx, zxr, zxl, halves)
+        z_hop(h, zi, zir, zil, whole)
+    zgr = z_own(grd, zg, right["z"])
+    zgl = z_own(grd, zg, left["z"])
 
     k = z // 2
     total = zi[0]
@@ -306,8 +317,6 @@
                 psel[...], block, preferred_element_type=jnp.float32
             ).astype(jnp.bfloat16)
 
-    col_a, col_b = pl.ds(0, HALF), pl.ds(HALF, HALF)
-
     def y_send(buf):
         ra = send(buf.at[y, :, col_a], buf.at[y, :, col_a], right["y"])
         lb = send(buf.at[y, :, col_b], buf.at[y, :, col_b], left["y"])
@@ -324,21 +333,21 @@
 
     compact(zx, xa)
     yx = y_send(xa)
-    z_hop(1, zg, zgr, zgl)
+    z_hop(1, zg, zgr, zgl, halves)
     s_xm, s_xp, s_x2 = 2 * xm + c, 2 * xp + c, 2 * ((x + 2) % 4) + c
     wra.wait_recv()
-    wfa = send(wbuf.at[s_xm, half_a], wbuf.at[s_xm, half_a], right["x"])
+    wfa = [send(wbuf.at[s_xm, q], wbuf.at[s_xm, q], right["x"]) for q in quarters_a]
     ws.append(send(wbuf.at[s_xm, half_a], wbuf.at[s_xm, half_a], sib))
     wlb.wait_recv()
-    wfb = send(wbuf.at[s_xp, half_b], wbuf.at[s_xp, half_b], left["x"])
+    wfb = [send(wbuf.at[s_xp, q], wbuf.at[s_xp, q], left["x"]) for q in quarters_b]
     ws.append(send(wbuf.at[s_xp, half_b], wbuf.at[s_xp, half_b], sib))
     fs.wait_recv()
     chip_state(f_own, f_sib, f_chip, c == 1)
     far_send(f_chip, f_far, 0, 1)
-    z_hop(2, zg, zgr, zgl)
-    z_hop(3, zg, zgr, zgl)
+    z_hop(2, zg, zgr, zgl, halves)
+    z_hop(3, zg, zgr, zgl, halves)
     yxf = y_relay(xa, yx[0], yx[1])
-    z_hop(4, zg, zgr, zgl)
+    z_hop(4, zg, zgr, zgl, halves)
     compact(zg, ga)
     yg = y_send(ga)
     yx[2].wait_recv()
@@ -351,21 +360,16 @@
     yxf[1].wait_recv()
 
     def add_in(shard):
-        cols = pl.ds(pl.multiple_of(shard * W_ROWS, W_ROWS), W_ROWS)
-        left_op = xa[:, :, cols].reshape(4 * CAP, W_ROWS)
+        cols = pl.ds(pl.multiple_of(shard * W_COLS, W_COLS), W_COLS)
+        left_op = xa[:, :, cols].reshape(4 * CAP, W_COLS)
         for at, wide in ((0, 256), (256, 256), (512, 256), (768, 256), (1024, 128)):
-            pre[:, at : at + wide] += jnp.dot(
-                left_op, wbuf[shard, :, at : at + wide], preferred_element_type=jnp.float32
-            )
+            pre[:, at : at + wide] += mm(left_op, wbuf[shard, at : at + wide, :], nt)
 
     def add_out(shard):
-        cols = pl.ds(pl.multiple_of(shard * W_ROWS, W_ROWS), W_ROWS)
-        left_op = ga[:, :, cols].reshape(4 * CAP, W_ROWS)
-        for at, wide in ((0, 256), (256, 256), (512, 128)):
-            ugr[:, at : at + wide] += jnp.dot(
-                left_op, wbuf[shard, :, N_IN + at : N_IN + at + wide],
-                preferred_element_type=jnp.float32,
-            )
+        cols = pl.ds(pl.multiple_of(shard * W_COLS, W_COLS), W_COLS)
+        left_op = ga[:, :, cols].reshape(4 * CAP, W_COLS)
+        for at, wide in ((0, 256), (256, 256), (512, 64)):
+            ugr[:, at : at + wide] += mm(left_op, wbuf[shard, N_IN + at : N_IN + at + wide, :], nt)
 
     for copy in ws:
         copy.wait_recv()
@@ -385,10 +389,11 @@
     def _(i):
         add_out((2 * (x + 3) + i) % 8)
 
-    wfa.wait_recv()
-    ws.append(send(wbuf.at[s_x2, half_a], wbuf.at[s_x2, half_a], sib))
-    wfb.wait_recv()
-    ws.append(send(wbuf.at[s_x2, half_b], wbuf.at[s_x2, half_b], sib))
+    for n in range(2):
+        wfa[n].wait_recv()
+        ws.append(send(wbuf.at[s_x2, quarters_a[n]], wbuf.at[s_x2, quarters_a[n]], sib))
+        wfb[n].wait_recv()
+        ws.append(send(wbuf.at[s_x2, quarters_b[n]], wbuf.at[s_x2, quarters_b[n]], sib))
     add_in(s_x2)
     add_out(s_x2)
     for copy in ws[ws_done:]:
@@ -422,105 +427,130 @@
 
     def to_dx(shard):
         for at in (0, 256, 512):
-            cols = pl.ds(pl.multiple_of(shard * W_ROWS + at, 256), 256)
-            part = lax.dot_general(
-                ggu[...], wbuf[shard, at : at + 256, 0:N_IN], (((1,), (1,)), ((), ())),
-                preferred_element_type=jnp.float32,
-            )
-            dxs[:, :, cols] = part.astype(jnp.bfloat16).reshape(4, CAP, 256)
-
-    ext_b = pl.ds(HALF, D_EXT - HALF)
-
-    @pl.loop(0, 4)
-    def _(i):
-        to_dx(i)
-
-    ha = send(dxs.at[y2, :, col_a], yha, right["y"])
-    fma = send(dxs.at[ym, :, col_a], yfp.at[:, col_a], left["y"])
-
-    @pl.loop(4, 8)
-    def _(i):
-        to_dx(i)
-
-    hb = send(dxs.at[y2, :, ext_b], yhb, left["y"])
-    fpb = send(dxs.at[yp, :, ext_b], yfm.at[:, ext_b], right["y"])
-
-    def add_rows(dst, add, lo, n):
-        @pl.loop(0, n // 128)
+            cols = pl.ds(pl.multiple_of(shard * W_COLS + at, 256), 256)
+            part = mm(ggu[...], wbuf[shard, 0:N_IN, at : at + 256], nn)
+            dxs[:, :, cols] = part.astype(bf16).reshape(4, CAP, 256)
+
+    span = 2 * W_COLS
+    group_a = [pl.ds(g * span, W_COLS) for g in range(4)]
+    group_b = [pl.ds(g * span + W_COLS, W_COLS + (128 if g == 3 else 0)) for g in range(4)]
+    group = [pl.ds(g * span, span + (128 if g == 3 else 0)) for g in range(4)]
+    far_a, far_b, to_left, to_right, last_a, last_b = {}, {}, {}, {}, {}, {}
+
+    def dx_group(g):
+        @pl.loop(2 * g, 2 * g + 2)
         def _(i):
-            to = pl.ds(pl.multiple_of(lo + i * 128, 128), 128)
-            fr = pl.ds(pl.multiple_of(i * 128, 128), 128)
-            dst[:, to] = (
-                dst[:, to].astype(jnp.float32) + add[:, fr].astype(jnp.float32)
-            ).astype(jnp.bfloat16)
-
-    ha.wait_recv()
-    add_rows(dxs.at[yp], yha, 0, HALF)
-    fpa = send(dxs.at[yp, :, col_a], yfm.at[:, col_a], right["y"])
-    hb.wait_recv()
-    add_rows(dxs.at[ym], yhb, HALF, D_EXT - HALF)
-    fmb = send(dxs.at[ym, :, ext_b], yfp.at[:, ext_b], left["y"])
+            to_dx(i)
+
+        a, b = group_a[g], group_b[g]
+        far_a[g] = send(dxs.at[y2, :, a], yh.at[:, a], right["y"])
+        far_b[g] = send(dxs.at[y2, :, b], yh.at[:, b], left["y"])
+
+    def direct(g):
+        a, b = group_a[g], group_b[g]
+        to_right[g] = send(dxs.at[yp, :, b], yfm.at[:, b], right["y"])
+        to_left[g] = send(dxs.at[ym, :, a], yfp.at[:, a], left["y"])
+
+    def add_cols(dst, cols):
+        @pl.loop(0, cols.size // 128)
+        def _(i):
+            at = pl.ds(pl.multiple_of(cols.start + i * 128, 128), 128)
+            dst[:, at] = (dst[:, at].astype(f32) + yh[:, at].astype(f32)).astype(bf16)
+
+    def relayed(g):
+        a, b = group_a[g], group_b[g]
+        far_a[g].wait_recv()
+        add_cols(dxs.at[yp], a)
+        last_a[g] = send(dxs.at[yp, :, a], yfm.at[:, a], right["y"])
+        far_b[g].wait_recv()
+        add_cols(dxs.at[ym], b)
+        last_b[g] = send(dxs.at[ym, :, b], yfp.at[:, b], left["y"])
+
+    def spread(cols, wide, gated):
+        part = dxs[y, :, cols].astype(f32) + yfp[:, cols].astype(f32) + yfm[:, cols].astype(f32)
+        if gated:
+            part = part * gate_slot
+        cz[:, :, cols] = mm(psel[...], part.astype(bf16), tn).astype(bf16).reshape(8, TOK, wide)
+
+    z_right, z_left = {}, {}
+
+    def y_end(g):
+        for copies in (to_left, to_right, last_a, last_b):
+            copies[g].wait_recv()
+
+        @pl.loop(0, span // 512)
+        def _(i):
+            spread(pl.ds(pl.multiple_of(g * span + i * 512, 512), 512), 512, True)
+
+        if g == 3:
+            spread(pl.ds(D, 128), 128, False)
+        z_right[g] = [send(cz.at[(z + 4) % 8, :, group[g]], zr.at[0, :, group[g]], right["z"])]
+        z_left[g] = [send(cz.at[(z + 5) % 8, :, group[g]], zl.at[0, :, group[g]], left["z"])]
+
+    def z_add(at, src, cols):
+        cz[at, :, cols] = (cz[at, :, cols].astype(f32) + src[:, cols].astype(f32)).astype(bf16)
+
+    def z_step(g, h):
+        cols = group[g]
+        at = (z + 4 - h) % 8
+        z_right[g][h - 1].wait_recv()
+        z_add(at, zr.at[h - 1], cols)
+        z_right[g].append(send(cz.at[at, :, cols], zr.at[h, :, cols], right["z"]))
+        if h < 3:
+            at = (z + 5 + h) % 8
+            z_left[g][h - 1].wait_recv()
+            z_add(at, zl.at[h - 1], cols)
+            z_left[g].append(send(cz.at[at, :, cols], zl.at[h, :, cols], left["z"]))
+
+    def z_end(g):
+        cols = group[g]
+        z_left[g][2].wait_recv()
+        z_right[g][3].wait_recv()
+        out[:, cols] = (
+            cz[z, :, cols].astype(f32) + zr[3, :, cols].astype(f32) + zl[2, :, cols].astype(f32)
+        )
+
+    dx_group(0)
+    direct(0)
+    dx_group(1)
+    relayed(0)
+    direct(1)
+    dx_group(2)
+    relayed(1)
+    direct(2)
+    dx_group(3)
+    relayed(2)
+    direct(3)
     far_state(f_chip, f_far, f_sib, 0, 1, c == 1)
-    attention_main()
+    attention_main(0, 2)
+    y_end(0)
+    relayed(3)
+    attention_main(2, 4)
     bs = send(b_own, b_sib, sib)
+    z_step(0, 1)
+    y_end(1)
     bs.wait_recv()
     chip_state(b_own, b_sib, b_chip, c == 0)
     far_send(b_chip, b_far, 6, -1)
-    for copy in (fma, fpb, fpa, fmb):
-        copy.wait_recv()
-
-    def spread(cols, wide, gated):
-        part = dxs[y, :, cols].astype(jnp.float32) + yfp[:, cols].astype(jnp.float32)
-        part = part + yfm[:, cols].astype(jnp.float32)
-        if gated:
-            part = part * gate_slot
-        back = lax.dot_general(
-            psel[...], part.astype(jnp.bfloat16), (((0,), (0,)), ((), ())),
-            preferred_element_type=jnp.float32,
-        )
-        cz[:, :, cols] = back.astype(jnp.bfloat16).reshape(8, TOK, wide)
-
-    @pl.loop(0, D // 512)
-    def _(i):
-        spread(pl.ds(pl.multiple_of(i * 512, 512), 512), 512, True)
-
-    spread(pl.ds(D, 128), 128, False)
-
-    parts = (col_a, ext_b)
-
-    def z_first(dst, dev, at):
-        return [send(cz.at[at, :, p], dst.at[0, :, p], dev) for p in parts]
-
-    zrc = [z_first(zr, right["z"], (z + 4) % 8)]
-    zlc = [z_first(zl, left["z"], (z + 5) % 8)]
+    z_step(0, 2)
+    z_step(1, 1)
+    z_step(0, 3)
+    y_end(2)
+    z_step(1, 2)
+    z_end(0)
+    z_step(2, 1)
+    z_step(1, 3)
+    y_end(3)
+    z_step(2, 2)
+    z_end(1)
+    z_step(3, 1)
+    z_step(2, 3)
+    z_step(3, 2)
     far_state(b_chip, b_far, b_sib, 6, -1, c == 0)
+    z_end(2)
+    z_step(3, 3)
     attention_last()
-    for h in range(1, 4):
-        nr, nl = [], []
-        for n, p in enumerate(parts):
-            at = (z + 4 - h) % 8
-            zrc[h - 1][n].wait_recv()
-            cz[at, :, p] = (
-                cz[at, :, p].astype(jnp.float32) + zr[h - 1, :, p].astype(jnp.float32)
-            ).astype(jnp.bfloat16)
-            nr.append(send(cz.at[at, :, p], zr.at[h, :, p], right["z"]))
-            if h < 3:
-                at = (z + 5 + h) % 8
-                zlc[h - 1][n].wait_recv()
-                cz[at, :, p] = (
-                    cz[at, :, p].astype(jnp.float32) + zl[h - 1, :, p].astype(jnp.float32)
-                ).astype(jnp.bfloat16)
-                nl.append(send(cz.at[at, :, p], zl.at[h, :, p], left["z"]))
-        zrc.append(nr)
-        zlc.append(nl)
-    for n, p in enumerate(parts):
-        zlc[2][n].wait_recv()
-        zrc[3][n].wait_recv()
-        out[:, p] = (
-            cz[z, :, p].astype(jnp.float32)
-            + zr[3, :, p].astype(jnp.float32)
-            + zl[2, :, p].astype(jnp.float32)
-        )
+    z_end(3)
 
     score = out[:, D:D_EXT]
     gate = gates[...]
@@ -530,7 +560,7 @@
     @pl.loop(0, D // 512)
     def _(i):
         cols = pl.ds(pl.multiple_of(i * 512, 512), 512)
-        to_hidden = mm(l_high, router[cols, :], nt) + mm(l_low, router[cols, :], nt)
+        to_hidden = mm(l_high, router[:, cols], nn) + mm(l_low, router[:, cols], nn)
         gh[:, cols] = (out[:, cols] + to_hidden).astype(bf16)
 
     for copy in started:
@@ -572,7 +602,7 @@
     bf16, f32 = jnp.bfloat16, jnp.float32
     vmem, smem = (pl.BlockSpec(memory_space=m) for m in (pltpu.VMEM, pltpu.SMEM))
     hbm = pl.BlockSpec(memory_space=pl.ANY)
-    n_copies = 68
+    n_copies = 118
     grads = jax.ShapeDtypeStruct((2, BLOCK, 2 * HEAD), bf16)
     states = pltpu.VMEM((2, 2, HEAD, HEAD), f32)
     return pl.pallas_call(
@@ -586,23 +616,22 @@
         scratch_shapes=[
             pltpu.VMEM((2, BLOCK, 128), f32),
             pltpu.VMEM((TOK, 128), f32),
+            pltpu.VMEM((2, TOK, 128), f32),
             pltpu.VMEM((TOK, D), bf16),
             pltpu.VMEM((8, 128), f32),
             pltpu.VMEM((TOK, 128), f32),
-            pltpu.VMEM((3, W_ROWS, H_MAIN + H_TAIL), bf16),
             pltpu.VMEM((TOK, D_EXT), f32),
-            pltpu.VMEM((8, W_ROWS, N_ALL), bf16),
+            pltpu.VMEM((8, N_ALL, W_COLS), bf16),
             pltpu.VMEM((8, TOK, D), bf16),
             pltpu.VMEM((8, TOK, D), bf16),
             pltpu.VMEM((8, 8, 128), f32),
             pltpu.VMEM((4, CAP, D), bf16),
             pltpu.VMEM((4, CAP, D), bf16),
             pltpu.VMEM((4 * CAP, N_IN), f32),
-            pltpu.VMEM((4 * CAP, N_ALL - N_IN), f32),
+            pltpu.VMEM((4 * CAP, U_PAD), f32),
             pltpu.VMEM((4 * CAP, N_IN), bf16),
             pltpu.VMEM((4, CAP, D_EXT), bf16),
-            pltpu.VMEM((CAP, HALF), bf16),
-            pltpu.VMEM((CAP, D_EXT - HALF), bf16),
+            pltpu.VMEM((CAP, D_EXT), bf16),
             pltpu.VMEM((CAP, D_EXT), bf16),
             pltpu.VMEM((CAP, D_EXT), bf16),
             pltpu.VMEM((8, TOK, D_EXT), bf16),
@@ -618,7 +647,7 @@
             pltpu.VMEM((2, BLOCK, 2 * HEAD), f32),
             pltpu.SemaphoreType.DMA((n_copies,)),
             pltpu.SemaphoreType.DMA((n_copies,)),
-            pltpu.SemaphoreType.DMA((3,)),
+            pltpu.SemaphoreType.DMA((5,)),
             pltpu.SemaphoreType.DMA((12,)),
             pltpu.SemaphoreType.DMA((12,)),
         ],
@@ -654,8 +683,8 @@
 ):
     rollouts, positions, width = hidden_in.shape
     objective, *rest = all_blocks(
-        hidden_in.reshape(TOK, width), moe_probe.reshape(TOK, width), router_weight,
-        routes.reshape(TOK, 2), gate_weight, up_weight, down_weight,
+        hidden_in.reshape(TOK, width), moe_probe.reshape(TOK, width), router_weight.T,
+        routes.transpose(0, 2, 1), *(w.transpose(0, 2, 1) for w in (gate_weight, up_weight, down_weight)),
         queries, key_rows, value_rows, attn_probe, decay_rate, norm_gain.reshape(1, -1),
         rollout_logprob, trainer_logprob, advantage, clip_low, clip_high,
     )

time: 192 us -> 176 us (0.917)
  Pallas kernels: 182 us -> 174 us
  local copies, waits for them, and re-layouts: 7.9 us -> 0 us
    pallas_call x1, Pallas kernels: 180 us -> 172 us  [all_blocks(): pl.pallas_call(kernel, out_shape=[jax.ShapeDtypeStruct((2, BLOCK), f32),...]
    unnamed x10 -> x0, local copies, waits for them, and re-layouts: 6.54 us -> none
where the time goes in v4:
time: 176 us
  Pallas kernels  174 us (99%)
  between operations  1.94 us (1%)
    pallas_call x1, Pallas kernels, all_blocks(): pl.pallas_call(kernel, out_shape=[jax.ShapeDtypeStruct((2, BLOCK), f32),...  172 us

profile of v4, /device:TPU:6, one launch (start us, length us, event | category | flops | bytes accessed | tf_op | source)
XLA Modules:
  0.0 175.5 jit_solution(10021855950903010076)
XLA Ops:
  1.9 171.6 %all_blocks.1 = (f32[2,256]{1,0:T(2,128)}, bf16[16,6144]{1,0:T(8,128)(2,1)}, bf16[2,256,256]{2,1,0:T(8,128)(2,1)}, bf16[2,256,256]{2,1,0:T(8,128)(2,1)}, bf16[2,256,256]{2,1,0:T(8,128)(2,1)}) custom-call(bf16[16,6144]{1,0:T(8,128)(2,1)} %bitcast.12, bf16[16,6144]{1,0:T(8,128)(2,1)} %bitcast.13, bf16[4,6144]{1,0:T(4,128)(2,1)} %bitcast.15, ...), custom_call_target="tpu_custom_call" | custom-call | flops 12000000000 | bytes 40000000 | tf_op jit(solution)/shard_map/all_blocks/pallas_call | solution.py:608
  173.5 2.0 %results.1 = (f32[2,256]{1,0:T(2,128)}, bf16[16,6144]{1,0:T(8,128)(2,1)}, bf16[2,256,256]{2,1,0:T(8,128)(2,1)}, bf16[2,256,256]{2,1,0:T(8,128)(2,1)}, bf16[2,256,256]{2,1,0:T(8,128)(2,1)}) custom-call(f32[2,256]{1,0:T(2,128)} %get-tuple-element.15.refs_0_, bf16[16,6144]{1,0:T(8,128)(2,1)} %get-tuple-element.16.refs_1_, ...), custom_call_target="tpu_custom_call" | custom-call | tf_op jit(solution)/shard_map/results/pallas_call | solution.py:590

commit v5 on v4

--- a/solution.py
+++ b/solution.py
@@ -249,31 +249,6 @@
     zir = [[send(info, zi.at[z], right["z"])]]
     zil = [[send(info, zi.at[z], left["z"])]]
 
-    ratio = jnp.exp(train_lp[...] - roll_lp[...])
-    ratio = jnp.minimum(jnp.maximum(ratio, low[0]), high[0])
-    coeff = -(ratio * adv[...]) / 2.0
-    obj[...] = coeff * train_lp[...]
-    for r in range(2):
-        for part in range(2):
-            row = jnp.broadcast_to(coeff[r : r + 1, 128 * part : 128 * part + 128], (128, 128))
-            col = jnp.sum(jnp.where(eye, row, 0.0), axis=1, keepdims=True)
-            coef[r, 128 * part : 128 * part + 128, :] = jnp.broadcast_to(col, (128, 128))
-    here = pl.ds(pl.multiple_of(8 * (4 * z + y), 8), 8)
-    for r in range(2):
-        coef_tok[8 * r : 8 * r + 8, :] = coef[r, here, :]
-
-    @pl.loop(0, D // 512)
-    def _(i):
-        cols = pl.ds(pl.multiple_of(i * 512, 512), 512)
-        grad = moe[:, cols].astype(f32) * coef_tok[:, 0:1]
-        grd[:, cols] = grad.astype(bf16)
-        zg[z, :, cols] = grad.astype(bf16)
-
-    pre[...] = jnp.zeros_like(pre)
-    ugr[...] = jnp.zeros_like(ugr)
-    summaries()
-    fs = send(f_own, f_sib, sib)
-
     def z_hop(h, buf, rights, lefts, pieces):
         nr, nl = [], []
         for n, p in enumerate(pieces):
@@ -293,8 +268,6 @@
     for h in range(1, 5):
         z_hop(h, zx, zxr, zxl, halves)
         z_hop(h, zi, zir, zil, whole)
-    zgr = z_own(grd, zg, right["z"])
-    zgl = z_own(grd, zg, left["z"])
 
     k = z // 2
     total = zi[0]
@@ -333,6 +306,33 @@
 
     compact(zx, xa)
     yx = y_send(xa)
+
+    ratio = jnp.exp(train_lp[...] - roll_lp[...])
+    ratio = jnp.minimum(jnp.maximum(ratio, low[0]), high[0])
+    coeff = -(ratio * adv[...]) / 2.0
+    obj[...] = coeff * train_lp[...]
+    for r in range(2):
+        for part in range(2):
+            row = jnp.broadcast_to(coeff[r : r + 1, 128 * part : 128 * part + 128], (128, 128))
+            col = jnp.sum(jnp.where(eye, row, 0.0), axis=1, keepdims=True)
+            coef[r, 128 * part : 128 * part + 128, :] = jnp.broadcast_to(col, (128, 128))
+    here = pl.ds(pl.multiple_of(8 * (4 * z + y), 8), 8)
+    for r in range(2):
+        coef_tok[8 * r : 8 * r + 8, :] = coef[r, here, :]
+
+    @pl.loop(0, D // 512)
+    def _(i):
+        cols = pl.ds(pl.multiple_of(i * 512, 512), 512)
+        grad = moe[:, cols].astype(f32) * coef_tok[:, 0:1]
+        grd[:, cols] = grad.astype(bf16)
+        zg[z, :, cols] = grad.astype(bf16)
+
+    zgr = z_own(grd, zg, right["z"])
+    zgl = z_own(grd, zg, left["z"])
+    pre[...] = jnp.zeros_like(pre)
+    ugr[...] = jnp.zeros_like(ugr)
+    summaries()
+    fs = send(f_own, f_sib, sib)
     z_hop(1, zg, zgr, zgl, halves)
     s_xm, s_xp, s_x2 = 2 * xm + c, 2 * xp + c, 2 * ((x + 2) % 4) + c
     wra.wait_recv()
@@ -519,36 +519,38 @@
     relayed(1)
     direct(2)
     dx_group(3)
+    far_state(f_chip, f_far, f_sib, 0, 1, c == 1)
+    attention_main(0, 1)
+    y_end(0)
+    attention_main(1, 2)
+    z_step(0, 1)
     relayed(2)
     direct(3)
-    far_state(f_chip, f_far, f_sib, 0, 1, c == 1)
-    attention_main(0, 2)
-    y_end(0)
+    attention_main(2, 3)
+    z_step(0, 2)
+    y_end(1)
+    attention_main(3, 4)
+    bs = send(b_own, b_sib, sib)
+    z_step(0, 3)
+    z_step(1, 1)
     relayed(3)
-    attention_main(2, 4)
-    bs = send(b_own, b_sib, sib)
-    z_step(0, 1)
-    y_end(1)
     bs.wait_recv()
     chip_state(b_own, b_sib, b_chip, c == 0)
     far_send(b_chip, b_far, 6, -1)
-    z_step(0, 2)
-    z_step(1, 1)
-    z_step(0, 3)
+    z_end(0)
+    z_step(1, 2)
     y_end(2)
-    z_step(1, 2)
-    z_end(0)
+    z_step(1, 3)
     z_step(2, 1)
-    z_step(1, 3)
+    z_end(1)
+    z_step(2, 2)
     y_end(3)
-    z_step(2, 2)
-    z_end(1)
+    z_step(2, 3)
     z_step(3, 1)
-    z_step(2, 3)
+    z_end(2)
     z_step(3, 2)
+    z_step(3, 3)
     far_state(b_chip, b_far, b_sib, 6, -1, c == 0)
-    z_end(2)
-    z_step(3, 3)
     attention_last()
     z_end(3)
 

time: 176 us -> 171 us (0.972)
  Pallas kernels: 174 us -> 169 us
    pallas_call x1, Pallas kernels: 172 us -> 167 us  [all_blocks(): pl.pallas_call(kernel, out_shape=[jax.ShapeDtypeStruct((2, BLOCK), f32),...]
where the time goes in v5:
time: 171 us
  Pallas kernels  169 us (99%)
  between operations  1.94 us (1%)
    pallas_call x1, Pallas kernels, all_blocks(): pl.pallas_call(kernel, out_shape=[jax.ShapeDtypeStruct((2, BLOCK), f32),...  167 us

profile of v5, /device:TPU:6, one launch (start us, length us, event | category | flops | bytes accessed | tf_op | source)
XLA Modules:
  0.0 170.9 jit_solution(12035959998771542408)
XLA Ops:
  1.9 166.9 %all_blocks.1 = (f32[2,256]{1,0:T(2,128)}, bf16[16,6144]{1,0:T(8,128)(2,1)}, bf16[2,256,256]{2,1,0:T(8,128)(2,1)}, bf16[2,256,256]{2,1,0:T(8,128)(2,1)}, bf16[2,256,256]{2,1,0:T(8,128)(2,1)}) custom-call(bf16[16,6144]{1,0:T(8,128)(2,1)} %bitcast.12, bf16[16,6144]{1,0:T(8,128)(2,1)} %bitcast.13, bf16[4,6144]{1,0:T(4,128)(2,1)} %bitcast.15, ...), custom_call_target="tpu_custom_call" | custom-call | flops 12000000000 | bytes 40000000 | tf_op jit(solution)/shard_map/all_blocks/pallas_call | solution.py:610
  168.9 2.0 %results.1 = (f32[2,256]{1,0:T(2,128)}, bf16[16,6144]{1,0:T(8,128)(2,1)}, bf16[2,256,256]{2,1,0:T(8,128)(2,1)}, bf16[2,256,256]{2,1,0:T(8,128)(2,1)}, bf16[2,256,256]{2,1,0:T(8,128)(2,1)}) custom-call(f32[2,256]{1,0:T(2,128)} %get-tuple-element.15.refs_0_, bf16[16,6144]{1,0:T(8,128)(2,1)} %get-tuple-element.16.refs_1_, ...), custom_call_target="tpu_custom_call" | custom-call | tf_op jit(solution)/shard_map/results/pallas_call | solution.py:592

commit v6 on v5

--- a/solution.py
+++ b/solution.py
@@ -28,7 +28,7 @@
     tok, moe, router, route, gate_w, up_w, down_w, qr, kr, vr, pr, rate, gain,
     roll_lp, train_lp, adv, low, high,
     obj, gh, gq, gk, gv,
-    coef, coef_tok, route_tok, grd, info, gates, out,
+    coef, coef_tok, route_tok, grd, info, gates, logit,
     wbuf, zx, zg, zi, xa, ga, pre, ugr, ggu, dxs, yh, yfp, yfm, cz, zr, zl, psel,
     f_own, f_sib, f_chip, b_own, b_sib, b_chip, f_far, b_far, state, dk_part, dv_part,
     ssem, rsem, lsem, xss, xrs,
@@ -431,14 +431,18 @@
             part = mm(ggu[...], wbuf[shard, 0:N_IN, at : at + 256], nn)
             dxs[:, :, cols] = part.astype(bf16).reshape(4, CAP, 256)
 
-    span = 2 * W_COLS
-    group_a = [pl.ds(g * span, W_COLS) for g in range(4)]
-    group_b = [pl.ds(g * span + W_COLS, W_COLS + (128 if g == 3 else 0)) for g in range(4)]
-    group = [pl.ds(g * span, span + (128 if g == 3 else 0)) for g in range(4)]
+    shards = [(6, 8), (4, 6), (2, 4), (0, 2)]
+    group_a, group_b, group = [], [], []
+    for lo, hi in shards:
+        first, end = lo * W_COLS, D_EXT if hi == 8 else hi * W_COLS
+        middle = (lo + hi) * W_COLS // 2
+        group_a.append(pl.ds(first, middle - first))
+        group_b.append(pl.ds(middle, end - middle))
+        group.append(pl.ds(first, end - first))
     far_a, far_b, to_left, to_right, last_a, last_b = {}, {}, {}, {}, {}, {}
 
     def dx_group(g):
-        @pl.loop(2 * g, 2 * g + 2)
+        @pl.loop(*shards[g])
         def _(i):
             to_dx(i)
 
@@ -478,11 +482,11 @@
         for copies in (to_left, to_right, last_a, last_b):
             copies[g].wait_recv()
 
-        @pl.loop(0, span // 512)
+        @pl.loop(2 * shards[g][0], 2 * shards[g][1])
         def _(i):
-            spread(pl.ds(pl.multiple_of(g * span + i * 512, 512), 512), 512, True)
-
-        if g == 3:
+            spread(pl.ds(pl.multiple_of(i * 384, 128), 384), 384, True)
+
+        if g == 0:
             spread(pl.ds(D, 128), 128, False)
         z_right[g] = [send(cz.at[(z + 4) % 8, :, group[g]], zr.at[0, :, group[g]], right["z"])]
         z_left[g] = [send(cz.at[(z + 5) % 8, :, group[g]], zl.at[0, :, group[g]], left["z"])]
@@ -502,13 +506,23 @@
             z_add(at, zl.at[h - 1], cols)
             z_left[g].append(send(cz.at[at, :, cols], zl.at[h, :, cols], left["z"]))
 
+    def span_of(g):
+        return (shards[g][1] - shards[g][0]) * W_COLS
+
     def z_end(g):
         cols = group[g]
         z_left[g][2].wait_recv()
         z_right[g][3].wait_recv()
-        out[:, cols] = (
+        whole_sum = (
             cz[z, :, cols].astype(f32) + zr[3, :, cols].astype(f32) + zl[2, :, cols].astype(f32)
         )
+        if g == 0:
+            score, share = whole_sum[:, span_of(g) :], gates[...]
+            logit[...] = share * (score - jnp.sum(share * score, axis=1, keepdims=True))
+        l_high, l_low = parts_of(logit[:, 0:4])
+        cols = pl.ds(cols.start, span_of(g))
+        to_hidden = mm(l_high, router[:, cols], nn) + mm(l_low, router[:, cols], nn)
+        gh[:, cols] = (whole_sum[:, : span_of(g)] + to_hidden).astype(bf16)
 
     dx_group(0)
     direct(0)
@@ -554,17 +568,6 @@
     attention_last()
     z_end(3)
 
-    score = out[:, D:D_EXT]
-    gate = gates[...]
-    logit = gate * (score - jnp.sum(gate * score, axis=1, keepdims=True))
-    l_high, l_low = parts_of(logit[:, 0:4])
-
-    @pl.loop(0, D // 512)
-    def _(i):
-        cols = pl.ds(pl.multiple_of(i * 512, 512), 512)
-        to_hidden = mm(l_high, router[:, cols], nn) + mm(l_low, router[:, cols], nn)
-        gh[:, cols] = (out[:, cols] + to_hidden).astype(bf16)
-
     for copy in started:
         copy.wait_send()
     far_send(f_chip, f_far, 0, 1, finish=True)
@@ -622,7 +625,7 @@
             pltpu.VMEM((TOK, D), bf16),
             pltpu.VMEM((8, 128), f32),
             pltpu.VMEM((TOK, 128), f32),
-            pltpu.VMEM((TOK, D_EXT), f32),
+            pltpu.VMEM((TOK, 128), f32),
             pltpu.VMEM((8, N_ALL, W_COLS), bf16),
             pltpu.VMEM((8, TOK, D), bf16),
             pltpu.VMEM((8, TOK, D), bf16),

time: 171 us -> 171 us (level)
  no operation moved by 1% of the time
where the time goes in v6:
time: 171 us
  Pallas kernels  169 us (99%)
  between operations  1.94 us (1%)
    pallas_call x1, Pallas kernels, all_blocks(): pl.pallas_call(kernel, out_shape=[jax.ShapeDtypeStruct((2, BLOCK), f32),...  167 us

profile of v6, /device:TPU:6, one launch (start us, length us, event | category | flops | bytes accessed | tf_op | source)
XLA Modules:
  0.0 171.2 jit_solution(12331403895239349719)
XLA Ops:
  1.9 167.2 %all_blocks.1 = (f32[2,256]{1,0:T(2,128)}, bf16[16,6144]{1,0:T(8,128)(2,1)}, bf16[2,256,256]{2,1,0:T(8,128)(2,1)}, bf16[2,256,256]{2,1,0:T(8,128)(2,1)}, bf16[2,256,256]{2,1,0:T(8,128)(2,1)}) custom-call(bf16[16,6144]{1,0:T(8,128)(2,1)} %bitcast.12, bf16[16,6144]{1,0:T(8,128)(2,1)} %bitcast.13, bf16[4,6144]{1,0:T(4,128)(2,1)} %bitcast.15, ...), custom_call_target="tpu_custom_call" | custom-call | flops 12000000000 | bytes 40000000 | tf_op jit(solution)/shard_map/all_blocks/pallas_call | solution.py:613
  169.2 2.0 %results.1 = (f32[2,256]{1,0:T(2,128)}, bf16[16,6144]{1,0:T(8,128)(2,1)}, bf16[2,256,256]{2,1,0:T(8,128)(2,1)}, bf16[2,256,256]{2,1,0:T(8,128)(2,1)}, bf16[2,256,256]{2,1,0:T(8,128)(2,1)}) custom-call(f32[2,256]{1,0:T(2,128)} %get-tuple-element.15.refs_0_, bf16[16,6144]{1,0:T(8,128)(2,1)} %get-tuple-element.16.refs_1_, ...), custom_call_target="tpu_custom_call" | custom-call | tf_op jit(solution)/shard_map/results/pallas_call | solution.py:595
